TPU v7x, 512 devices: a whole 4x8x8 slice. The times are simulated.
512 devices in a mesh: sub: 16 (over z, core), tile: 32 (over y, x).
Axes of the slice: x: 4, y: 8, z: 8, core: 2. Of those that a mesh axis runs over, the one named last changes fastest.
Arguments:
- echoes: float32 [32, 32, 128], P('sub', 'tile'), may hold values from -6 to 6
- pulse_offset: float32 [32, 32], P('sub', 'tile'), may hold values from 0 to 1
- range_gates: int32 [32, 32, 64], P('sub', 'tile'), may hold values from 0 to 511
- visible: int32 [32, 256], P('sub', 'tile'), may hold values 0 or 1
Outputs:
- images: float32 [32, 256, 128, 256], P('sub', 'tile')
- peak: float32 [256, 128, 128], P('tile', 'sub')
All inputs are finite; a program needn't handle non-finite values. No bound on the sum of `visible` on one device may be relied on, other than what follows from the above.
Results may differ from a plain program's by a relative error of at most 0.0037.
Values sent between devices are 32-bit elements; how exact they have to be, the bound alone decides.
No kernel may reach another device: no remote copies, remote signals or barrier semaphores. Data moves between devices by JAX's collectives and lax.ppermute only.
A program may use at most 64 MiB of HBM per device.

v0:
```python
import math

import jax
import jax.numpy as jnp
from jax import lax
from jax.sharding import PartitionSpec as P

PULSE_H = 32
FREQS = 64
PIX = 128
GATES = 512


grid_cols = 16
two_pi = 2.0 * math.pi


def shifted(block, axis, distance):
    devices = range(lax.axis_size(axis))
    route = [((i - distance) % len(devices), i) for i in devices]
    return lax.ppermute(block, axis, route)


def make_right(sine_wave):
    pixels = jnp.arange(PIX, dtype=jnp.float32)
    phase_grid = sine_wave[:, None] * pixels[None, :]
    real_part = jnp.cos(phase_grid).astype(jnp.bfloat16)
    imag_part = jnp.sin(phase_grid).astype(jnp.bfloat16)
    upper = jnp.concatenate([real_part, imag_part], axis=1)
    lower = jnp.concatenate([-imag_part, real_part], axis=1)
    return jnp.concatenate([upper, lower], axis=0)


def make_base(cosine_wave):
    pixels = jnp.arange(PIX, dtype=jnp.float32)
    base_phase = cosine_wave[None, :] * pixels[:, None]
    return (jnp.cos(base_phase), jnp.sin(base_phase))


def make_left(
    echo_real, echo_imag, cosine_wave, sine_wave, base_cos, base_sin, tile_number, norm_scale
):
    column = (tile_number % grid_cols * PIX - 8 * PIX).astype(jnp.float32)
    row_start = (tile_number // grid_cols * PIX - 4 * PIX).astype(jnp.float32)
    offset_phase = cosine_wave * column + sine_wave * row_start
    offset_cos = jnp.cos(offset_phase)
    offset_sin = jnp.sin(offset_phase)
    turned_real = norm_scale * (echo_real * offset_cos - echo_imag * offset_sin)
    turned_imag = norm_scale * (echo_real * offset_sin + echo_imag * offset_cos)
    real_part = turned_real[None, :] * base_cos - turned_imag[None, :] * base_sin
    imag_part = turned_real[None, :] * base_sin + turned_imag[None, :] * base_cos
    return jnp.concatenate([real_part, imag_part], axis=1).astype(jnp.bfloat16)


def on_device(echoes, pulse_offset, range_gates, visible):
    half_dev = echoes.shape[0]
    tile_dev = visible.shape[1]
    sub_count = lax.axis_size("sub")
    half_total = half_dev * sub_count
    first_half = lax.axis_index("sub") * half_dev
    first_tile = lax.axis_index("tile") * tile_dev
    half_numbers = first_half + jnp.arange(half_dev, dtype=jnp.int32)
    angles = two_pi * (half_numbers.astype(jnp.float32)[:, None] + pulse_offset) / half_total
    waves = 0.5 + range_gates.astype(jnp.float32) / GATES
    shown = visible.astype(jnp.float32)
    half_count = echoes.shape[0]
    norm_scale = (2.0 * PULSE_H * FREQS) ** (-0.5)
    echo_piece = lax.all_gather(echoes, "tile", axis=1, tiled=True)
    wave_piece = lax.all_gather(waves, "tile", axis=1, tiled=True)
    angle_piece = lax.all_gather(angles, "tile", axis=1, tiled=True)
    stacked = []
    for half_slot in range(half_count):
        cosine_wave = (wave_piece[half_slot] * jnp.cos(angle_piece[half_slot])[:, None]).reshape(-1)
        sine_wave = (wave_piece[half_slot] * jnp.sin(angle_piece[half_slot])[:, None]).reshape(-1)
        echo_real = echo_piece[half_slot][:, :FREQS].reshape(-1)
        echo_imag = echo_piece[half_slot][:, FREQS:].reshape(-1)
        right_side = make_right(sine_wave)
        base_cos, base_sin = make_base(cosine_wave)
        tile_terms = []
        for tile_slot in range(tile_dev):

            def compute(
                echo_real=echo_real,
                echo_imag=echo_imag,
                cosine_wave=cosine_wave,
                sine_wave=sine_wave,
                base_cos=base_cos,
                base_sin=base_sin,
                right_side=right_side,
                tile_slot=tile_slot,
            ):
                left_side = make_left(
                    echo_real,
                    echo_imag,
                    cosine_wave,
                    sine_wave,
                    base_cos,
                    base_sin,
                    first_tile + tile_slot,
                    norm_scale,
                )
                return jnp.dot(left_side, right_side, preferred_element_type=jnp.float32)

            tile_term = compute()
            tile_terms.append(tile_term)
        stacked.append(jnp.stack(tile_terms))
    half_images = jnp.stack(stacked)
    half_images = half_images * shown[:, :, None, None]
    following = shifted(half_images[0], "sub", -1)
    successors = jnp.concatenate([half_images[1:half_dev], following[None]], axis=0)
    images = half_images + successors
    power_map = images[..., :PIX] ** 2 + images[..., PIX:] ** 2
    local_peak = jnp.max(power_map, axis=0)
    full_peak = lax.pmax(local_peak, "sub")
    row_count = PIX // sub_count
    peak = lax.dynamic_slice_in_dim(full_peak, lax.axis_index("sub") * row_count, row_count, 1)
    return (images, peak)


def solution(mesh):
    in_specs = (P("sub", "tile", None), P("sub", "tile"), P("sub", "tile", None), P("sub", "tile"))
    out_specs = (P("sub", "tile", None, None), P("tile", "sub", None))
    return jax.shard_map(
        on_device, mesh=mesh, in_specs=in_specs, out_specs=out_specs, check_vma=False
    )
```

profile of v0, /device:TPU:1, one launch (start us, length us, event | category | flops | bytes accessed | tf_op | source)
XLA Modules:
  0.0 301.1 jit_solution(487523907034118992)
XLA Ops:
  7.2 0.0 all-reduce.2.cloned.1.call-start
  7.3 0.7 multiply_bitcast_fusion
  8.0 29.8 %all-gather = f32[32,1,2]{2,1,0:T(1,128)S(1)} all-gather(f32[1,1,2]{2,1,0:T(1,128)S(1)} %multiply_bitcast_fusion), channel_id=1, replica_groups=mesh['sub'=16,'tile'=32] {'tile'}, dimensions={0}, use_global_device_ids=true | all-gather | bytes 264 | tf_op jit(solution)/shard_map/all_gather | solution.py:70
  37.8 0.1 copy.9
  37.9 0.1 sine_bitcast_fusion.1
  37.9 0.1 mul.1893
  38.0 0.1 mul.1894
  38.1 0.1 mul.1900
  38.1 0.1 mul.1901
  38.2 0.1 mul.2050
  38.3 0.1 mul.2051
  38.3 0.1 mul.2054
  38.4 0.1 mul.2055
  38.5 29.0 %all_gather.9 = f32[2,32,128]{2,0,1:T(2,128)S(1)} all-gather(f32[2,1,128]{2,0,1:T(2,128)} %bitcast.94), channel_id=1, replica_groups=mesh['sub'=16,'tile'=32] {'tile'}, dimensions={1}, use_global_device_ids=true | all-gather | bytes 33792 | tf_op jit(solution)/shard_map/all_gather | solution.py:68
  67.5 0.1 fusion.122
  67.6 0.1 reshape.961
  67.6 0.1 reshape.962
  67.7 0.1 fusion.123
  67.8 0.1 reshape.963
  67.9 0.1 reshape.964
  67.9 0.7 multiply_add_fusion.16
  68.6 28.6 %all_gather.10 = f32[2,32,64]{2,0,1:T(2,128)S(1)} all-gather(f32[2,1,64]{2,0,1:T(2,128)S(1)} %multiply_add_fusion.16), channel_id=1, replica_groups=mesh['sub'=16,'tile'=32] {'tile'}, dimensions={1}, use_global_device_ids=true | all-gather | bytes 16896 | tf_op jit(solution)/shard_map/all_gather | solution.py:69
  97.2 0.1 slice_reduce_fusion.1
  97.3 0.1 squeeze.11
  97.4 0.1 squeeze.26
  97.4 0.1 subtract_multiply_fusion
  97.5 4.5 %sine_convert_fusion.1 = (bf16[2048,128]{1,0:T(8,128)(2,1)S(1)}, bf16[2048,128]{1,0:T(8,128)(2,1)S(1)}) fusion(f32[2048]{0:T(1024)S(1)} %get-tuple-element.117), kind=kLoop, calls=%fused_computation.125 | loop fusion | flops 786432 | bytes 1056768 | tf_op jit(solution)/shard_map/convert_element_type | solution.py:28
  102.0 4.1 %fusion.70 = bf16[2048,128]{1,0:T(8,128)(2,1)S(1)} fusion(f32[2048]{0:T(1024)S(1)} %get-tuple-element.117), kind=kLoop, calls=%fused_computation.133 | loop fusion | flops 1310720 | bytes 532480 | tf_op jit(solution)/shard_map/neg | solution.py:30
  106.2 0.1 subtract_multiply_fusion.15
  106.2 0.1 subtract_multiply_fusion.7
  106.3 0.3 add_multiply_fusion.8
  106.6 0.3 add_multiply_fusion
  106.8 4.5 %sine_convert_fusion = (bf16[2048,128]{1,0:T(8,128)(2,1)S(1)}, bf16[2048,128]{1,0:T(8,128)(2,1)S(1)}) fusion(f32[2048]{0:T(1024)S(1)} %get-tuple-element.9), kind=kLoop, calls=%fused_computation.103 | loop fusion | flops 786432 | bytes 1056768 | tf_op jit(solution)/shard_map/convert_element_type | solution.py:28
  111.3 4.1 %fusion.71 = bf16[2048,128]{1,0:T(8,128)(2,1)S(1)} fusion(f32[2048]{0:T(1024)S(1)} %get-tuple-element.9), kind=kLoop, calls=%fused_computation.134 | loop fusion | flops 1310720 | bytes 532480 | tf_op jit(solution)/shard_map/neg | solution.py:30
  115.4 0.0 copy-done.1
  115.4 6.3 %subtract_convert_fusion.8 = (bf16[128,2048]{1,0:T(8,128)(2,1)S(1)}, bf16[128,2048]{1,0:T(8,128)(2,1)S(1)}, bf16[128,2048]{1,0:T(8,128)(2,1)S(1)}, bf16[128,2048...) fusion(f32[2048]{0:T(1024)S(1)} %get-tuple-element.12, ...), kind=kLoop, calls=%fused_computation.112 | loop fusion | flops 17039360 | bytes 8527872 | tf_op jit(solution)/shard_map/convert.16
  121.7 0.5 fusion.15
  122.2 0.5 fusion.14
  122.6 0.5 fusion.13
  123.1 0.5 fusion.12
  123.6 0.5 fusion.11
  124.1 0.5 fusion.10
  124.6 0.5 fusion.9
  125.1 0.5 fusion.8
  125.6 6.2 %subtract_convert_fusion = (bf16[128,2048]{1,0:T(8,128)(2,1)S(1)}, bf16[128,2048]{1,0:T(8,128)(2,1)S(1)}, bf16[128,2048]{1,0:T(8,128)(2,1)S(1)}, bf16[128,2048]{...) fusion(f32[2048]{0:T(1024)S(1)} %get-tuple-element.29, ...), kind=kLoop, calls=%fused_computation.90 | loop fusion | flops 17039360 | bytes 8527872 | tf_op jit(solution)/shard_map/convert
  131.8 0.4 fusion.7
  132.2 0.4 fusion.6
  132.7 0.4 fusion.5
  133.1 0.4 fusion.4
  133.6 0.4 fusion.3
  134.0 0.5 fusion.2
  134.5 0.5 fusion.1
  135.0 0.5 fusion
  135.5 0.3 maximum_multiply_fusion
  135.7 0.2 fusion.120
  135.9 25.8 %collective-permute-start = (f32[8,128,256]{2,1,0:T(8,128)S(1)}, f32[8,128,256]{2,1,0:T(8,128)S(1)}, u32[]{:S(2)}, u32[]{:S(2)}) collective-permute-start(f32[8,128,256]{2,1,0:T(8,128)S(1)} %get-tuple-element.11), channel_id=1, source_target_pairs={{32,0},{64,32},{96,64},{128,96},{160,128},{192,160},{224,192},{256... | collective-permute-start | bytes 3145736 | tf_op jit(solution)/shard_map/ppermute | solution.py:21
  161.7 13.5 %collective-permute-done = f32[8,128,256]{2,1,0:T(8,128)S(1)} collective-permute-done((f32[8,128,256]{2,1,0:T(8,128)S(1)}, f32[8,128,256]{2,1,0:T(8,128)S(1)}, u32[]{:S(2)}, u32[]{:S(2)}) %collective-permute-start) | collective-permute-done | bytes 1048608 | tf_op jit(solution)/shard_map/ppermute | solution.py:21
  175.2 0.3 maximum_add_fusion
  175.6 0.0 copy-start
  175.6 1.1 fusion.17
  176.7 0.0 all-reduce.2.cloned.1.call-update
  176.7 116.2 %all-reduce.2.cloned.1.call-done = f32[8,128,128]{2,1,0:T(8,128)} async-done(((f32[8,128,128]{2,1,0:T(8,128)}), f32[8,128,128]{2,1,0:T(8,128)}) %all-reduce.2.cloned.1.call-update) | async-done | bytes 524304 | tf_op jit(solution)/shard_map/pmax | solution.py:114
  292.9 1.4 constant_dynamic-slice_fusion
  294.3 0.0 copy-done
  (3 shorter events, 0.0 us)
Async XLA Ops:
  7.2 285.7 %all-reduce.2.cloned.1.call-start = ((), (), s32[]{:S(2)}) async-start(), calls=%async_computation | async-start | bytes 1048576 | tf_op jit(solution)/shard_map/pmax | solution.py:114
  67.7 47.7 %copy-start.1 = (s32[2,8]{1,0:T(2,128)S(1)}, s32[2,8]{1,0:T(2,128)}, u32[]{:S(2)}) copy-start(s32[2,8]{1,0:T(2,128)} %param.7) | copy-start | bytes 196
  135.9 39.3 %collective-permute-start = (f32[8,128,256]{2,1,0:T(8,128)S(1)}, f32[8,128,256]{2,1,0:T(8,128)S(1)}, u32[]{:S(2)}, u32[]{:S(2)}) collective-permute-start(f32[8,128,256]{2,1,0:T(8,128)S(1)} %get-tuple-element.11), channel_id=1, source_target_pairs={{32,0},{64,32},{96,64},{128,96},{160,128},{192,160},{224,192},{256... | collective-permute-start | bytes 3145736 | tf_op jit(solution)/shard_map/ppermute | solution.py:21
  175.6 118.7 %copy-start = (f32[2,8,128,256]{3,2,1,0:T(8,128)}, f32[2,8,128,256]{3,2,1,0:T(8,128)S(1)}, u32[]{:S(2)}) copy-start(f32[2,8,128,256]{3,2,1,0:T(8,128)S(1)} %maximum_add_fusion) | copy-start | bytes 6291460
Sparse Core Ops, SparseCore 0:
  176.8 116.0 all-reduce.1
where the time goes:
time: 301 us
  waiting for transfers between devices  130 us (43%)
  blocking collectives  87.4 us (29%)
  other arithmetic  33.3 us (11%)
  starting transfers between devices  25.8 us (9%)
  between operations  14.5 us (5%)
  matrix products  7.47 us (2%)
    pmax x1, waiting for transfers between devices, on_device(): full_peak = lax.pmax(local_peak, 'sub')  116 us
    all_gather x1, blocking collectives, on_device(): angle_piece = lax.all_gather(angles, 'tile', axis=1, tiled=True)  29.8 us
    all_gather x1, blocking collectives, on_device(): echo_piece = lax.all_gather(echoes, 'tile', axis=1, tiled=True)  29 us
    all_gather x1, blocking collectives, on_device(): wave_piece = lax.all_gather(waves, 'tile', axis=1, tiled=True)  28.6 us
    ppermute x1, starting transfers between devices, shifted(): return lax.ppermute(block, axis, route)  25.8 us
    ppermute x1, waiting for transfers between devices, shifted(): return lax.ppermute(block, axis, route)  13.5 us
    another operation x2, other arithmetic  12.5 us
    convert_element_type x2, other arithmetic, make_right(): imag_part = jnp.sin(phase_grid).astype(jnp.bfloat16)  8.92 us
  transfers between devices with their start and end apart: 2, of which 2 were waited for; matrix products, arithmetic and copies ran while one was open for 0% of the time, Pallas kernels for 0%

commit v1 on v0

v1 whole, which is shorter than its diff:
```python
import functools
import math

import jax
import jax.numpy as jnp
from jax import lax
from jax.experimental import pallas as pl
from jax.experimental.pallas import tpu as pltpu
from jax.sharding import PartitionSpec as P

PULSE_H = 32
FREQS = 64
PIX = 128
GATES = 512
LANES = 128
CHUNKS = PULSE_H * FREQS // LANES
TILES_DEV = 8
DEPTH = 256

two_pi = 2.0 * math.pi
F32 = jnp.float32
BF16 = jnp.bfloat16


def sincos(x):
    n = jnp.round(x * F32(2.0 / math.pi))
    r = ((x - n * F32(1.5703125)) - n * F32(4.837512969970703125e-4)) - n * F32(7.54978995489188216e-8)
    r2 = r * r
    s = r + r * r2 * (F32(-1.6666654611e-1) + r2 * (F32(8.3321608736e-3) + r2 * F32(-1.9515295891e-4)))
    c = (1.0 - 0.5 * r2) + r2 * r2 * (F32(4.166664568298827e-2) + r2 * (F32(-1.388731625493765e-3) + r2 * F32(2.443315711809948e-5)))
    q = n.astype(jnp.int32)
    odd = (q & 1) == 1
    cos = jnp.where(odd, s, c)
    sin = jnp.where(odd, c, s)
    cos = jnp.where(((q + 1) & 2) == 2, -cos, cos)
    sin = jnp.where((q & 2) == 2, -sin, sin)
    return cos, sin


def times(a, b):
    return a[0] * b[0] - a[1] * b[1], a[0] * b[1] + a[1] * b[0]


def turned_both(a, b):
    p, q, r, t = a[0] * b[0], a[1] * b[1], a[1] * b[0], a[0] * b[1]
    return (p - q, r + t), (p + q, r - t)


def pack_kernel(sub_ref, echo_ref, offset_ref, gates_ref, shown_ref, out_ref):
    half = (2 * sub_ref[0] + lax.broadcasted_iota(jnp.int32, (2, FREQS), 0)).astype(F32)
    offset = jnp.broadcast_to(offset_ref[...], (2, FREQS))
    angle = two_pi * (half + offset) / 32
    wave = 0.5 + gates_ref[...].astype(F32) / GATES
    cos, sin = sincos(angle)
    waves = jnp.concatenate([wave * cos, wave * sin], axis=1)
    out_ref[...] = jnp.zeros_like(out_ref)
    out_ref[0:1, :] = waves[0:1]
    out_ref[1:2, :] = echo_ref[0:1, :]
    out_ref[2:3, :] = waves[1:2]
    out_ref[3:4, :] = echo_ref[1:2, :]
    out_ref[4:6, 0:TILES_DEV] = shown_ref[...].astype(F32)


def pack(sub, echoes, offset, gates, shown):
    vmem = pl.BlockSpec(memory_space=pltpu.VMEM)
    return pl.pallas_call(
        pack_kernel,
        out_shape=jax.ShapeDtypeStruct((8, LANES), F32),
        in_specs=[pl.BlockSpec(memory_space=pltpu.SMEM)] + [vmem] * 4,
        out_specs=vmem,
    )(sub, echoes, offset, gates, shown)


def spread_kernel(own_ref, next_ref, out_ref):
    tile = jnp.concatenate([own_ref[0:4, :], next_ref[0:4, :]], axis=0)
    out_ref[...] = jnp.broadcast_to(tile[None], out_ref.shape)


def spread(own, following):
    vmem = pl.BlockSpec(memory_space=pltpu.VMEM)
    return pl.pallas_call(
        spread_kernel,
        out_shape=jax.ShapeDtypeStruct((32, 8, LANES), F32),
        in_specs=[vmem] * 2,
        out_specs=vmem,
    )(own, following)


def row(ref, at):
    return jnp.broadcast_to(ref[pl.ds(at, 1), :], (8, LANES))


def image_kernel(place_ref, g_ref, own_ref, next_ref, images_ref, keep_ref, send_ref,
                 left_ref, right_ref, wave_ref, table_ref, prod_ref):
    tile_index = place_ref[0]
    core = place_ref[1]
    x_first = ((tile_index % 2) * 1024 - 1024).astype(F32)
    y_first = ((tile_index // 2) * 128 - 512).astype(F32)
    scale = F32((2.0 * PULSE_H * FREQS) ** -0.5)
    low = lax.broadcasted_iota(jnp.int32, (16, LANES), 1) < FREQS
    sigma = lax.broadcasted_iota(jnp.int32, (8, LANES), 0).astype(F32) - 3.5

    def halved(at):
        m = g_ref[pl.ds(at, 32, stride=8), :]
        t = pltpu.roll(m, FREQS, 1)
        return jnp.where(low, m[:16], t[16:]), jnp.where(low, t[:16], m[16:])

    def build(half):
        ca, sa = halved(2 * half)
        er, ei = halved(2 * half + 1)
        wave_ref[0:16, :] = ca
        wave_ref[16:32, :] = sa

        def put(slot, v):
            table_ref[slot * 32: slot * 32 + 16, :] = v[0]
            table_ref[slot * 32 + 16: slot * 32 + 32, :] = v[1]

        e4 = sincos(ca * 4.0)
        e8 = times(e4, e4)
        v = e4
        for m in range(4):
            put(m, v)
            if m < 3:
                v = times(v, e8)
        e32 = times(v, e4)
        e64 = times(e32, e32)
        v = e32
        for j in range(4):
            put(4 + j, v)
            if j < 3:
                v = times(v, e64)
        e4 = sincos(sa * 4.0)
        e8 = times(e4, e4)
        v = e4
        for m in range(8):
            put(8 + m, v)
            if m < 7:
                v = times(v, e8)
        for block in range(2):
            phase = ca * (x_first + (255.5 + 512.0 * block)) + sa * (y_first + 63.5)
            put(16 + block, times((er * scale, ei * scale), sincos(phase)))

        def chunk(c, carry):
            def entry(slot):
                return row(table_ref, slot * 32 + c), row(table_ref, slot * 32 + 16 + c)

            lanes = pl.ds(pl.multiple_of(c * LANES, LANES), LANES)
            w = sincos(row(wave_ref, c) * sigma)
            for j in range(4):
                a = times(w, entry(4 + j))
                rows = [None] * 8
                for m in range(4):
                    rows[4 + m], rows[3 - m] = turned_both(a, entry(m))
                for b in range(0, 8, 2):
                    at = j * 64 + b * 8
                    for part in range(2):
                        left_ref[part * DEPTH + at: part * DEPTH + at + 16, lanes] = jnp.concatenate(
                            [rows[b][part], rows[b + 1][part]], axis=0).astype(BF16)
            v = sincos(row(wave_ref, 16 + c) * sigma)
            for block in range(2):
                a = times(v, entry(16 + block))
                rows = [None] * 16
                for m in range(8):
                    rows[8 + m], rows[7 - m] = turned_both(a, entry(8 + m))
                for b in range(0, 16, 2):
                    at = block * 256 + b * 8
                    for part in range(2):
                        right_ref[part * 128 + at: part * 128 + at + 16, lanes] = jnp.concatenate(
                            [rows[b][part], rows[b + 1][part]], axis=0).astype(BF16)
            return carry

        lax.fori_loop(0, CHUNKS, chunk, 0)

    def product():
        prod_ref[...] = lax.dot_general(left_ref[...], right_ref[...], (((1,), (1,)), ((), ())),
                                        preferred_element_type=F32)

    def flip(v):
        at = lax.broadcasted_iota(jnp.int32, v.shape, 0)
        v = pltpu.roll(v, 4, 0)
        v = jnp.where((at & 2) == 0, pltpu.roll(v, 6, 0), pltpu.roll(v, 2, 0))
        return jnp.where((at & 1) == 0, pltpu.roll(v, 7, 0), pltpu.roll(v, 1, 0))

    def weight(half, tile):
        ref, at = (own_ref, 4 + half) if half < 2 else (next_ref, 4)
        return ref[at:at + 1, tile:tile + 1]

    def parts(half, block, quarter, r):
        rows = pl.ds(pl.multiple_of(quarter * 128 + r * 8, 8), 8)
        rows2 = pl.ds(pl.multiple_of(DEPTH + quarter * 128 + r * 8, 8), 8)
        pr = prod_ref[rows, block * 256: block * 256 + 128]
        pi = prod_ref[rows, block * 256 + 128: block * 256 + 256]
        qr = prod_ref[rows2, block * 256: block * 256 + 128]
        qi = prod_ref[rows2, block * 256 + 128: block * 256 + 256]
        up = jnp.broadcast_to(weight(half, block * 4 + 2 + quarter), (8, LANES))
        down = jnp.broadcast_to(weight(half, block * 4 + 1 - quarter), (8, LANES))
        return (pr - qi) * up, (pi + qr) * up, flip(pr + qi) * down, flip(pi - qr) * down

    def gather_half(half):
        for block in range(2):
            for quarter in range(2):
                for side in range(2):
                    pass

                def body(r, carry):
                    ur, ui, dr, di = parts(half, block, quarter, r)
                    for tile, at, re, im in (
                        (block * 4 + 2 + quarter, r, ur, ui),
                        (block * 4 + 1 - quarter, 15 - r, dr, di),
                    ):
                        rows = pl.ds(pl.multiple_of(at * 8, 8), 8)
                        if half == 0:
                            images_ref[0, tile, rows, 0:128] = re
                            images_ref[0, tile, rows, 128:256] = im
                        elif half == 1:
                            images_ref[0, tile, rows, 0:128] += re
                            images_ref[0, tile, rows, 128:256] += im
                            images_ref[1, tile, rows, 0:128] = re
                            images_ref[1, tile, rows, 128:256] = im
                        else:
                            re = images_ref[1, tile, rows, 0:128] + re
                            im = images_ref[1, tile, rows, 128:256] + im
                            images_ref[1, tile, rows, 0:128] = re
                            images_ref[1, tile, rows, 128:256] = im
                    return carry

                lax.fori_loop(0, 16, body, 0)

    for half in range(3):
        build(half)
        product()
        gather_half(half)

    for tile in range(TILES_DEV):
        def peaks(z, carry):
            both = []
            for c in range(2):
                rows = pl.ds(pl.multiple_of(z * 16 + c * 8, 8), 8)
                power = [images_ref[s, tile, rows, 0:128] ** 2 + images_ref[s, tile, rows, 128:256] ** 2
                         for s in range(2)]
                both.append(jnp.maximum(power[0], power[1]))
            keep_ref[z, tile] = jnp.where(core == 0, both[0], both[1])
            send_ref[z, tile] = jnp.where(core == 0, both[1], both[0])
            return carry

        lax.fori_loop(0, 8, peaks, 0)


def image(place, gathered, own, following):
    vmem = pl.BlockSpec(memory_space=pltpu.VMEM)
    piece = jax.ShapeDtypeStruct((8, TILES_DEV, 8, LANES), F32)
    return pl.pallas_call(
        image_kernel,
        out_shape=(jax.ShapeDtypeStruct((2, TILES_DEV, PIX, 2 * PIX), F32), piece, piece),
        in_specs=[pl.BlockSpec(memory_space=pltpu.SMEM)] + [vmem] * 3,
        out_specs=(vmem, vmem, vmem),
        scratch_shapes=[
            pltpu.VMEM((2 * DEPTH, PULSE_H * FREQS), BF16),
            pltpu.VMEM((512, PULSE_H * FREQS), BF16),
            pltpu.VMEM((32, LANES), F32),
            pltpu.VMEM((18 * 32, LANES), F32),
            pltpu.VMEM((2 * DEPTH, 512), F32),
        ],
        compiler_params=pltpu.CompilerParams(vmem_limit_bytes=40 * 1024 * 1024),
    )(place, gathered, own, following)


def on_device(echoes, pulse_offset, range_gates, visible):
    sub = lax.axis_index("sub")
    tile = lax.axis_index("tile")
    subs = lax.axis_size("sub")
    own = pack(sub[None].astype(jnp.int32), echoes[:, 0], pulse_offset, range_gates[:, 0], visible)
    following = lax.ppermute(own, "sub", [((i + 1) % subs, i) for i in range(subs)])
    gathered = lax.all_to_all(spread(own, following), "tile", 0, 0, tiled=True)
    place = jnp.stack([tile, sub % 2]).astype(jnp.int32)
    images, keep, send = image(place, gathered.reshape(256, LANES), own, following)
    other = lax.ppermute(send, "sub", [(i, i ^ 1) for i in range(subs)])
    both = jnp.maximum(keep, other)
    groups = [[2 * z + c for z in range(subs // 2)] for c in range(2)]
    pieces = lax.all_to_all(both, "sub", 0, 0, tiled=True, axis_index_groups=groups)
    return images, jnp.max(pieces, axis=0)


def solution(mesh):
    in_specs = (P("sub", "tile", None), P("sub", "tile"), P("sub", "tile", None), P("sub", "tile"))
    out_specs = (P("sub", "tile", None, None), P("tile", "sub", None))
    return jax.shard_map(
        on_device, mesh=mesh, in_specs=in_specs, out_specs=out_specs, check_vma=False
    )
```

time: 301 us -> 89.7 us (0.30)
  waiting for transfers between devices: 130 us -> 11.4 us
  blocking collectives: 87.4 us -> 14.8 us
  Pallas kernels: 0 us -> 34.9 us
  other arithmetic: 33.3 us -> 0.75 us
  between operations: 14.5 us -> 0.67 us
  matrix products: 7.47 us -> 0 us
    pmax x1 -> x0, waiting for transfers between devices: 116 us -> none  [on_device(): full_peak = lax.pmax(local_peak, 'sub')]
    all_gather x3 -> x0, blocking collectives: 87.4 us -> none  [the longest x1 29.8 us: on_device(): angle_piece = lax.all_gather(angles, 'tile', axis=1, tiled=True)]
    pallas_call x0 -> x3, Pallas kernels: none -> 34.9 us  [the longest x1 32 us: image(): pl.pallas_call(image_kernel, out_shape=(jax.ShapeDtypeStruct((2, TILES_DE...]
    all_to_all x0 -> x1, blocking collectives: none -> 14.8 us  [on_device(): lax.all_to_all(both, 'sub', 0, 0, tiled=True, axis_index_groups=groups)]
    another operation x2 -> x1, other arithmetic: 12.5 us -> 0.08 us  [on_device(): place = jnp.stack([tile, sub % 2]).astype(jnp.int32)]
    ppermute x1 -> x2, waiting for transfers between devices: 13.5 us -> 2.17 us  [the longest x1 1.14 us: on_device(): other = lax.ppermute(send, 'sub', [(i, i ^ 1) for i in range(subs)])]
    all_to_all x0 -> x1, waiting for transfers between devices: none -> 9.26 us  [on_device(): gathered = lax.all_to_all(spread(own, following), 'tile', 0, 0, tiled=True)]
    ppermute x1 -> x2, starting transfers between devices: 25.8 us -> 16.7 us  [the longest x1 9.87 us: on_device(): other = lax.ppermute(send, 'sub', [(i, i ^ 1) for i in range(subs)])]
  transfers between devices with their start and end apart: 2 -> 3, of which waited for: 2 -> 3; matrix products, arithmetic and copies ran while one was open for 0% -> 0% of each run, Pallas kernels for 0% -> 0%
where the time goes in v1:
time: 89.7 us; the launch traced here: 89.3 us
  Pallas kernels  34.9 us (39%)
  starting transfers between devices  23.5 us (26%)
  blocking collectives  14.8 us (16%)
  waiting for transfers between devices  11.4 us (13%)
  local copies, waits for them, and re-layouts  3.26 us (4%)
    pallas_call x1, Pallas kernels, image(): pl.pallas_call(image_kernel, out_shape=(jax.ShapeDtypeStruct((2, TILES_DE...  32 us
    all_to_all x1, blocking collectives, on_device(): lax.all_to_all(both, 'sub', 0, 0, tiled=True, axis_index_groups=groups)  14.8 us
    ppermute x1, starting transfers between devices, on_device(): other = lax.ppermute(send, 'sub', [(i, i ^ 1) for i in range(subs)])  9.87 us
    all_to_all x1, waiting for transfers between devices, on_device(): gathered = lax.all_to_all(spread(own, following), 'tile', 0, 0, tiled=True)  9.26 us
    ppermute x1, starting transfers between devices, on_device(): lax.ppermute(own, 'sub', [((i + 1) % subs, i) for i in range(subs)])  6.84 us
    all_to_all x1, starting transfers between devices, on_device(): gathered = lax.all_to_all(spread(own, following), 'tile', 0, 0, tiled=True)  6.77 us
    unnamed x7, local copies, waits for them, and re-layouts  3.26 us
  transfers between devices with their start and end apart: 3, of which 3 were waited for; matrix products, arithmetic and copies ran while one was open for 0% of the time, Pallas kernels for 0%

profile of v1, /device:TPU:1, one launch (start us, length us, event | category | flops | bytes accessed | tf_op | source)
XLA Modules:
  0.0 89.3 jit_solution(1240674391410133539)
XLA Ops:
  0.6 1.3 %copy.6.offset_ref = f32[2,1]{1,0:T(2,128)} copy(f32[2,1]{0,1:T(1,128)} %param.5) | data formatting | bytes 16 | tf_op args[1]
  1.9 1.5 %shard_map.59.own_ref = f32[8,128]{1,0:T(8,128)} custom-call(s32[1]{0:T(128)} %bitcast.2.sub_ref, f32[2,128]{1,0:T(2,128)} %bitcast.7, f32[2,1]{1,0:T(2,128)} %copy.6.offset_ref, s32[2,64]{1,0:T(2,128)} %bitcast.8, s32[2,8]{1,0:T(2,128)} %shown_ref.1), custom_call_target="tpu_custom_call" | custom-call | tf_op jit(solution)/shard_map/pallas_call | solution.py:66
  3.4 6.8 %collective-permute-start = (f32[8,128]{1,0:T(8,128)}, f32[8,128]{1,0:T(8,128)S(1)}, u32[]{:S(2)}, u32[]{:S(2)}) collective-permute-start(f32[8,128]{1,0:T(8,128)} %shard_map.59.own_ref), channel_id=1, source_target_pairs={{32,0},{64,32},{96,64},{128,96},{160,128},{192,160},{224,192},{256... | collective-permute-start | bytes 12296 | tf_op jit(solution)/shard_map/ppermute | solution.py:273
  10.2 1.0 %collective-permute-done.next_ref = f32[8,128]{1,0:T(8,128)S(1)} collective-permute-done((f32[8,128]{1,0:T(8,128)}, f32[8,128]{1,0:T(8,128)S(1)}, u32[]{:S(2)}, u32[]{:S(2)}) %collective-permute-start) | collective-permute-done | bytes 4128 | tf_op jit(solution)/shard_map/ppermute | solution.py:273
  11.3 0.0 copy-start.1
  11.3 0.6 copy-done.1
  11.9 1.4 %shard_map.60 = f32[32,8,128]{2,1,0:T(8,128)} custom-call(f32[8,128]{1,0:T(8,128)} %shard_map.59.own_ref, f32[8,128]{1,0:T(8,128)} %copy-done.1), custom_call_target="tpu_custom_call" | custom-call | tf_op jit(solution)/shard_map/pallas_call | solution.py:81
  13.2 6.8 %all-to-all-start = ((f32[32,8,128]{2,1,0:T(8,128)}), f32[32,8,128]{2,1,0:T(8,128)S(1)}, u32[]{:S(2)}, u32[]{:S(2)}) async-start(f32[32,8,128]{2,1,0:T(8,128)} %shard_map.60), calls=%async_computation | async-start | bytes 262144 | tf_op jit(solution)/shard_map/all_to_all | solution.py:274
  20.0 0.1 pad_add_fusion.place_ref
  20.1 9.3 %all-to-all-done = f32[32,8,128]{2,1,0:T(8,128)S(1)} async-done(((f32[32,8,128]{2,1,0:T(8,128)}), f32[32,8,128]{2,1,0:T(8,128)S(1)}, u32[]{:S(2)}, u32[]{:S(2)}) %all-to-all-start) | async-done | bytes 131104 | tf_op jit(solution)/shard_map/all_to_all | solution.py:274
  29.4 0.0 copy-start
  29.4 0.7 copy-done
  30.1 0.0 copy-start.2
  30.1 0.7 copy-done.2
  30.7 32.0 %shard_map.61 = (f32[2,8,128,256]{3,2,1,0:T(8,128)}, f32[8,8,8,128]{3,2,1,0:T(8,128)S(1)}, f32[8,8,8,128]{3,2,1,0:T(8,128)S(1)}) custom-call(s32[2]{0:T(128)S(1)} %pad_add_fusion.place_ref, f32[256,128]{1,0:T(8,128)S(1)} %bitcast.6, f32[8,128]{1,0:T(8,128)S(1)} %copy-done, f32[8,128]{1,0:T(8,128)S(1)} %copy-done.2), custom_call_target="tpu_custom_call" | custom-call | tf_op jit(solution)/shard_map/pallas_call | solution.py:252
  62.8 9.9 %collective-permute-start.1 = (f32[8,8,8,128]{3,2,1,0:T(8,128)S(1)}, f32[8,8,8,128]{3,2,1,0:T(8,128)S(1)}, u32[]{:S(2)}, u32[]{:S(2)}) collective-permute-start(f32[8,8,8,128]{3,2,1,0:T(8,128)S(1)} %get-tuple-element.7), channel_id=1, source_target_pairs={{0,32},{32,0},{64,96},{96,64},{128,160},{160,128},{192,224},{224,1... | collective-permute-start | bytes 786440 | tf_op jit(solution)/shard_map/ppermute | solution.py:277
  72.6 1.1 %collective-permute-done.1 = f32[8,8,8,128]{3,2,1,0:T(8,128)S(1)} collective-permute-done((f32[8,8,8,128]{3,2,1,0:T(8,128)S(1)}, f32[8,8,8,128]{3,2,1,0:T(8,128)S(1)}, u32[]{:S(2)}, u32[]{:S(2)}) %collective-permute-start.1) | collective-permute-done | bytes 262176 | tf_op jit(solution)/shard_map/ppermute | solution.py:277
  73.8 14.8 %all_to_all.10 = f32[8,8,8,128]{3,2,1,0:T(8,128)S(1)} all-to-all(f32[8,8,8,128]{3,2,1,0:T(8,128)S(1)} %max.3), channel_id=1, replica_groups={{0,64,128,192,256,320,384,448},{32,96,160,224,288,352,416,480},{1,65,12..., dimensions={0} | all-to-all | bytes 524288 | tf_op jit(solution)/shard_map/all_to_all | solution.py:280
  88.6 0.6 reduce_max.9
  (1 shorter events, 0.0 us)
Async XLA Ops:
  3.4 7.9 %collective-permute-start = (f32[8,128]{1,0:T(8,128)}, f32[8,128]{1,0:T(8,128)S(1)}, u32[]{:S(2)}, u32[]{:S(2)}) collective-permute-start(f32[8,128]{1,0:T(8,128)} %shard_map.59.own_ref), channel_id=1, source_target_pairs={{32,0},{64,32},{96,64},{128,96},{160,128},{192,160},{224,192},{256... | collective-permute-start | bytes 12296 | tf_op jit(solution)/shard_map/ppermute | solution.py:273
  11.3 0.6 copy-start.1
  13.2 16.1 %all-to-all-start = ((f32[32,8,128]{2,1,0:T(8,128)}), f32[32,8,128]{2,1,0:T(8,128)S(1)}, u32[]{:S(2)}, u32[]{:S(2)}) async-start(f32[32,8,128]{2,1,0:T(8,128)} %shard_map.60), calls=%async_computation | async-start | bytes 262144 | tf_op jit(solution)/shard_map/all_to_all | solution.py:274
  29.4 0.7 copy-start
  30.1 0.7 copy-start.2
  62.8 11.0 %collective-permute-start.1 = (f32[8,8,8,128]{3,2,1,0:T(8,128)S(1)}, f32[8,8,8,128]{3,2,1,0:T(8,128)S(1)}, u32[]{:S(2)}, u32[]{:S(2)}) collective-permute-start(f32[8,8,8,128]{3,2,1,0:T(8,128)S(1)} %get-tuple-element.7), channel_id=1, source_target_pairs={{0,32},{32,0},{64,96},{96,64},{128,160},{160,128},{192,224},{224,1... | collective-permute-start | bytes 786440 | tf_op jit(solution)/shard_map/ppermute | solution.py:277

commit v2 on v1

v2 whole, which is shorter than its diff:
```python
import functools
import math

import jax
import jax.numpy as jnp
from jax import lax
from jax.experimental import pallas as pl
from jax.experimental.pallas import tpu as pltpu
from jax.sharding import PartitionSpec as P

PULSE_H = 32
FREQS = 64
PIX = 128
GATES = 512
LANES = 128
CHUNKS = PULSE_H * FREQS // LANES
TILES_DEV = 8
DEPTH = 256

two_pi = 2.0 * math.pi
F32 = jnp.float32
BF16 = jnp.bfloat16


def sincos(x):
    n = jnp.round(x * F32(2.0 / math.pi))
    r = ((x - n * F32(1.5703125)) - n * F32(4.837512969970703125e-4)) - n * F32(7.54978995489188216e-8)
    r2 = r * r
    s = r + r * r2 * (F32(-1.6666654611e-1) + r2 * (F32(8.3321608736e-3) + r2 * F32(-1.9515295891e-4)))
    c = (1.0 - 0.5 * r2) + r2 * r2 * (F32(4.166664568298827e-2) + r2 * (F32(-1.388731625493765e-3) + r2 * F32(2.443315711809948e-5)))
    q = n.astype(jnp.int32)
    odd = (q & 1) == 1
    cos = jnp.where(odd, s, c)
    sin = jnp.where(odd, c, s)
    cos = jnp.where(((q + 1) & 2) == 2, -cos, cos)
    sin = jnp.where((q & 2) == 2, -sin, sin)
    return cos, sin


def times(a, b):
    return a[0] * b[0] - a[1] * b[1], a[0] * b[1] + a[1] * b[0]


def turned_both(a, b):
    p, q, r, t = a[0] * b[0], a[1] * b[1], a[1] * b[0], a[0] * b[1]
    return (p - q, r + t), (p + q, r - t)


def pack_kernel(place_ref, echo_ref, offset_ref, gates_ref, shown_ref, out_ref):
    first = lax.broadcasted_iota(jnp.int32, (2, FREQS), 0)
    half = (2 * place_ref[1] + first).astype(F32)
    offset = jnp.where(first == 0, offset_ref[0:1, 0:1], offset_ref[0:1, 1:2])
    angle = two_pi * (half + offset) / 32
    wave = 0.5 + gates_ref[...].astype(F32) / GATES
    cos, sin = sincos(angle)
    waves = jnp.concatenate([wave * cos, wave * sin], axis=1)
    out_ref[...] = jnp.zeros_like(out_ref)
    out_ref[0:1, :] = waves[0:1]
    out_ref[1:2, :] = echo_ref[0:1, :]
    out_ref[2:3, :] = waves[1:2]
    out_ref[3:4, :] = echo_ref[1:2, :]
    out_ref[4:6, 0:TILES_DEV] = shown_ref[...].astype(F32)


def pack(place, echoes, offset, gates, shown):
    vmem = pl.BlockSpec(memory_space=pltpu.VMEM)
    return pl.pallas_call(
        pack_kernel,
        out_shape=jax.ShapeDtypeStruct((8, LANES), F32),
        in_specs=[pl.BlockSpec(memory_space=pltpu.SMEM)] + [vmem] * 4,
        out_specs=vmem,
        compiler_params=pltpu.CompilerParams(vmem_limit_bytes=4 * 1024 * 1024),
    )(place, echoes, offset, gates, shown)


def spread_kernel(own_ref, next_ref, out_ref):
    shown = jnp.concatenate([own_ref[4:5, 0:FREQS], own_ref[5:6, 0:FREQS]], axis=1)
    tile = jnp.concatenate([own_ref[0:4, :], next_ref[0:2, :], shown, next_ref[4:5, :]], axis=0)
    out_ref[...] = jnp.broadcast_to(tile[None], out_ref.shape)


def spread(own, following):
    vmem = pl.BlockSpec(memory_space=pltpu.VMEM)
    return pl.pallas_call(
        spread_kernel,
        out_shape=jax.ShapeDtypeStruct((32, 8, LANES), F32),
        in_specs=[vmem] * 2,
        out_specs=vmem,
        compiler_params=pltpu.CompilerParams(vmem_limit_bytes=4 * 1024 * 1024),
    )(own, following)


def row(ref, at):
    return jnp.broadcast_to(ref[pl.ds(at, 1), :], (8, LANES))


def image_kernel(place_ref, g_ref, images_ref, keep_ref, send_ref,
                 left_ref, right_ref, wave_ref, table_ref, prod_ref, out_ref, sems):
    tile_index = place_ref[0]
    core = place_ref[1] % 2
    x_first = ((tile_index % 2) * 1024 - 1024).astype(F32)
    y_first = ((tile_index // 2) * 128 - 512).astype(F32)
    scale = F32((2.0 * PULSE_H * FREQS) ** -0.5)
    low = lax.broadcasted_iota(jnp.int32, (16, LANES), 1) < FREQS
    sigma = lax.broadcasted_iota(jnp.int32, (8, LANES), 0).astype(F32) - 3.5
    backwards = 7 - lax.broadcasted_iota(jnp.int32, (8, LANES), 0)

    def halved(at):
        m = g_ref[pl.ds(at, 32, stride=8), :]
        t = pltpu.roll(m, FREQS, 1)
        return jnp.where(low, m[:16], t[16:]), jnp.where(low, t[:16], m[16:])

    def build(half):
        ca, sa = halved(2 * half)
        er, ei = halved(2 * half + 1)
        wave_ref[0:16, :] = ca
        wave_ref[16:32, :] = sa

        def put(slot, v):
            table_ref[slot * 32: slot * 32 + 16, :] = v[0]
            table_ref[slot * 32 + 16: slot * 32 + 32, :] = v[1]

        e4 = sincos(ca * 4.0)
        e8 = times(e4, e4)
        v = e4
        for m in range(4):
            put(m, v)
            if m < 3:
                v = times(v, e8)
        e32 = times(v, e4)
        e64 = times(e32, e32)
        v = e32
        for j in range(4):
            put(4 + j, v)
            if j < 3:
                v = times(v, e64)
        e4 = sincos(sa * 4.0)
        e8 = times(e4, e4)
        v = e4
        for m in range(8):
            put(8 + m, v)
            if m < 7:
                v = times(v, e8)
        for block in range(2):
            phase = ca * (x_first + (255.5 + 512.0 * block)) + sa * (y_first + 63.5)
            put(16 + block, times((er * scale, ei * scale), sincos(phase)))

        def chunk(c, carry):
            def entry(slot):
                return row(table_ref, slot * 32 + c), row(table_ref, slot * 32 + 16 + c)

            w = sincos(row(wave_ref, c) * sigma)
            for j in range(4):
                a = times(w, entry(4 + j))
                rows = [None] * 8
                for m in range(4):
                    rows[4 + m], rows[3 - m] = turned_both(a, entry(m))
                for b in range(0, 8, 2):
                    at = j * 64 + b * 8
                    for part in range(2):
                        left_ref[c, part * DEPTH + at: part * DEPTH + at + 16, :] = jnp.concatenate(
                            [rows[b][part], rows[b + 1][part]], axis=0).astype(BF16)
            v = sincos(row(wave_ref, 16 + c) * sigma)
            for block in range(2):
                a = times(v, entry(16 + block))
                rows = [None] * 16
                for m in range(8):
                    rows[8 + m], rows[7 - m] = turned_both(a, entry(8 + m))
                for b in range(0, 16, 2):
                    at = block * 256 + b * 8
                    for part in range(2):
                        right_ref[c, part * 128 + at: part * 128 + at + 16, :] = jnp.concatenate(
                            [rows[b][part], rows[b + 1][part]], axis=0).astype(BF16)
            return carry

        lax.fori_loop(0, CHUNKS, chunk, 0)

    def product(half):
        left = jnp.concatenate([left_ref[c] for c in range(CHUNKS)], axis=1)
        right = jnp.concatenate([right_ref[c] for c in range(CHUNKS)], axis=1)
        prod_ref[half] = lax.dot_general(left, right, (((1,), (1,)), ((), ())), preferred_element_type=F32)

    def flip(v):
        return jnp.take_along_axis(v, backwards, axis=0)

    def weight(half, tile):
        lane = half * FREQS + tile if half < 2 else tile
        own = g_ref[pl.ds(tile_index * 8 + (6 if half < 2 else 7), 1), :]
        return jnp.broadcast_to(own[:, lane:lane + 1], (8, LANES))

    def out_copy(s, tile):
        return pltpu.make_async_copy(out_ref.at[s, tile], images_ref.at[s, tile], sems.at[s, tile])

    for half in range(3):
        build(half)
        product(half)

    for block in range(2):
        for quarter in range(2):
            upper, lower = block * 4 + 2 + quarter, block * 4 + 1 - quarter
            up = [weight(half, upper) for half in range(3)]
            down = [weight(half, lower) for half in range(3)]

            def finish(z, carry):
                power_up, power_down = [], []
                for c in range(2):
                    r = 2 * z + c
                    near = pl.ds(pl.multiple_of(quarter * 128 + r * 8, 8), 8)
                    far = pl.ds(pl.multiple_of(DEPTH + quarter * 128 + r * 8, 8), 8)
                    above, below = [], []
                    for half in range(3):
                        pr = prod_ref[half, near, block * 256: block * 256 + 128]
                        pi = prod_ref[half, near, block * 256 + 128: block * 256 + 256]
                        qr = prod_ref[half, far, block * 256: block * 256 + 128]
                        qi = prod_ref[half, far, block * 256 + 128: block * 256 + 256]
                        above.append(((pr - qi) * up[half], (pi + qr) * up[half]))
                        below.append(((pr + qi) * down[half], (pi - qr) * down[half]))
                    for sums, tile, at, power, turn in ((above, upper, r, power_up, False),
                                                        (below, lower, 15 - r, power_down, True)):
                        rows = pl.ds(pl.multiple_of(at * 8, 8), 8)
                        most = None
                        for s in range(2):
                            re, im = (sums[s][part] + sums[s + 1][part] for part in range(2))
                            if turn:
                                re, im = flip(re), flip(im)
                            out_ref[s, tile, rows, 0:128] = re
                            out_ref[s, tile, rows, 128:256] = im
                            now = re * re + im * im
                            most = now if most is None else jnp.maximum(most, now)
                        power.append(most)
                keep_ref[z, upper] = jnp.where(core == 0, power_up[0], power_up[1])
                send_ref[z, upper] = jnp.where(core == 0, power_up[1], power_up[0])
                keep_ref[7 - z, lower] = jnp.where(core == 0, power_down[1], power_down[0])
                send_ref[7 - z, lower] = jnp.where(core == 0, power_down[0], power_down[1])
                return carry

            lax.fori_loop(0, 8, finish, 0)
            for s in range(2):
                out_copy(s, upper).start()
                out_copy(s, lower).start()
    for s in range(2):
        for tile in range(TILES_DEV):
            out_copy(s, tile).wait()


def image(place, gathered):
    vmem = pl.BlockSpec(memory_space=pltpu.VMEM)
    piece = jax.ShapeDtypeStruct((8, TILES_DEV, 8, LANES), F32)
    return pl.pallas_call(
        image_kernel,
        out_shape=(jax.ShapeDtypeStruct((2, TILES_DEV, PIX, 2 * PIX), F32), piece, piece),
        in_specs=[pl.BlockSpec(memory_space=pltpu.SMEM), vmem],
        out_specs=(pl.BlockSpec(memory_space=pl.ANY), vmem, vmem),
        scratch_shapes=[
            pltpu.VMEM((CHUNKS, 2 * DEPTH, LANES), BF16),
            pltpu.VMEM((CHUNKS, 512, LANES), BF16),
            pltpu.VMEM((32, LANES), F32),
            pltpu.VMEM((18 * 32, LANES), F32),
            pltpu.VMEM((3, 2 * DEPTH, 512), F32),
            pltpu.VMEM((2, TILES_DEV, PIX, 2 * PIX), F32),
            pltpu.SemaphoreType.DMA((2, TILES_DEV)),
        ],
        compiler_params=pltpu.CompilerParams(vmem_limit_bytes=40 * 1024 * 1024),
    )(place, gathered)


def on_device(echoes, pulse_offset, range_gates, visible):
    sub = lax.axis_index("sub")
    tile = lax.axis_index("tile")
    subs = lax.axis_size("sub")
    place = jnp.stack([tile, sub]).astype(jnp.int32)
    own = pack(place, echoes[:, 0], pulse_offset.reshape(1, 2), range_gates[:, 0], visible)
    following = lax.ppermute(own, "sub", [((i + 1) % subs, i) for i in range(subs)])
    gathered = lax.all_to_all(spread(own, following), "tile", 0, 0, tiled=True)
    images, keep, send = image(place, gathered.reshape(256, LANES))
    other = lax.ppermute(send, "sub", [(i, i ^ 1) for i in range(subs)])
    both = jnp.maximum(keep, other)
    groups = [[2 * z + c for z in range(subs // 2)] for c in range(2)]
    pieces = lax.all_to_all(both, "sub", 0, 0, tiled=True, axis_index_groups=groups)
    return images, jnp.max(pieces, axis=0)


def solution(mesh):
    in_specs = (P("sub", "tile", None), P("sub", "tile"), P("sub", "tile", None), P("sub", "tile"))
    out_specs = (P("sub", "tile", None, None), P("tile", "sub", None))
    return jax.shard_map(
        on_device, mesh=mesh, in_specs=in_specs, out_specs=out_specs, check_vma=False
    )
```

time: 89.7 us -> 64.3 us (0.72)
  Pallas kernels: 34.9 us -> 10.5 us
  blocking collectives: 14.8 us -> 30.7 us
  waiting for transfers between devices: 11.4 us -> 1.96 us
  starting transfers between devices: 23.5 us -> 16.7 us
    pallas_call x1, Pallas kernels: 32 us -> 9.73 us  [image(): pl.pallas_call(image_kernel, out_shape=(jax.ShapeDtypeStruct((2, TILES_DE...]
    all_to_all x0 -> x1, blocking collectives: none -> 15.9 us  [on_device(): gathered = lax.all_to_all(spread(own, following), 'tile', 0, 0, tiled=True)]
    all_to_all x1 -> x0, waiting for transfers between devices: 9.26 us -> none  [on_device(): gathered = lax.all_to_all(spread(own, following), 'tile', 0, 0, tiled=True)]
    all_to_all x1 -> x0, starting transfers between devices: 6.77 us -> none  [on_device(): gathered = lax.all_to_all(spread(own, following), 'tile', 0, 0, tiled=True)]
    pallas_call x1, Pallas kernels: 1.37 us -> 0.08 us  [spread(): pl.pallas_call(spread_kernel, out_shape=jax.ShapeDtypeStruct((32, 8, LANE...]
    unnamed x7 -> x8, local copies, waits for them, and re-layouts: 3.26 us -> 2.69 us
  transfers between devices with their start and end apart: 3 -> 2, of which waited for: 3 -> 2; matrix products, arithmetic and copies ran while one was open for 0% -> 0% of each run, Pallas kernels for 0% -> 0%
where the time goes in v2:
time: 64.3 us; the launch traced here: 64 us
  blocking collectives  30.7 us (48%)
  starting transfers between devices  16.7 us (26%)
  Pallas kernels  10.5 us (16%)
  local copies, waits for them, and re-layouts  2.69 us (4%)
  waiting for transfers between devices  1.96 us (3%)
  other arithmetic  0.74 us (1%)
  between operations  0.66 us (1%)
    all_to_all x1, blocking collectives, on_device(): gathered = lax.all_to_all(spread(own, following), 'tile', 0, 0, tiled=True)  15.9 us
    all_to_all x1, blocking collectives, on_device(): lax.all_to_all(both, 'sub', 0, 0, tiled=True, axis_index_groups=groups)  14.8 us
    ppermute x1, starting transfers between devices, on_device(): other = lax.ppermute(send, 'sub', [(i, i ^ 1) for i in range(subs)])  9.88 us
    pallas_call x1, Pallas kernels, image(): pl.pallas_call(image_kernel, out_shape=(jax.ShapeDtypeStruct((2, TILES_DE...  9.73 us
    ppermute x1, starting transfers between devices, on_device(): lax.ppermute(own, 'sub', [((i + 1) % subs, i) for i in range(subs)])  6.84 us
    unnamed x8, local copies, waits for them, and re-layouts  2.69 us
  transfers between devices with their start and end apart: 2, of which 2 were waited for; matrix products, arithmetic and copies ran while one was open for 0% of the time, Pallas kernels for 0%

profile of v2, /device:TPU:1, one launch (start us, length us, event | category | flops | bytes accessed | tf_op | source)
XLA Modules:
  0.0 64.0 jit_solution(17088409671545610506)
XLA Ops:
  0.6 0.1 pad_add_fusion.place_ref
  0.7 0.0 copy-start
  0.7 0.7 %copy-done = f32[2,1,128]{2,1,0:T(1,128)S(1)} copy-done((f32[2,1,128]{2,1,0:T(1,128)S(1)}, f32[2,1,128]{2,1,0:T(1,128)}, u32[]{:S(2)}) %copy-start) | copy-done | bytes 1048
  1.4 0.0 copy-start.1
  1.4 0.7 %copy-done.1 = s32[2,1,64]{2,1,0:T(1,128)S(1)} copy-done((s32[2,1,64]{2,1,0:T(1,128)S(1)}, s32[2,1,64]{2,1,0:T(1,128)}, u32[]{:S(2)}) %copy-start.1) | copy-done | bytes 536
  2.1 0.0 copy-start.2
  2.1 0.7 %copy-done.2 = s32[2,8]{1,0:T(2,128)S(1)} copy-done((s32[2,8]{1,0:T(2,128)S(1)}, s32[2,8]{1,0:T(2,128)}, u32[]{:S(2)}) %copy-start.2) | copy-done | bytes 88
  2.7 0.0 copy-start.3
  2.8 0.7 %copy-done.3 = f32[2,1]{0,1:T(1,128)S(1)} copy-done((f32[2,1]{0,1:T(1,128)S(1)}, f32[2,1]{0,1:T(1,128)}, u32[]{:S(2)}) %copy-start.3) | copy-done | bytes 32
  3.4 0.7 %shard_map.59.own_ref = f32[8,128]{1,0:T(8,128)S(1)} custom-call(s32[2]{0:T(128)S(1)} %pad_add_fusion.place_ref, f32[2,128]{1,0:T(2,128)S(1)} %bitcast.7, f32[1,2]{1,0:T(1,128)S(1)} %bitcast.9, s32[2,64]{1,0:T(2,128)S(1)} %bitcast.8, s32[2,8]{1,0:T(2,128)S(1)} %copy-done.2), custom_call_target="tpu_custom_call" | custom-call | tf_op jit(solution)/shard_map/pallas_call | solution.py:67
  4.1 6.8 %collective-permute-start = (f32[8,128]{1,0:T(8,128)S(1)}, f32[8,128]{1,0:T(8,128)S(1)}, u32[]{:S(2)}, u32[]{:S(2)}) collective-permute-start(f32[8,128]{1,0:T(8,128)S(1)} %shard_map.59.own_ref), channel_id=1, source_target_pairs={{32,0},{64,32},{96,64},{128,96},{160,128},{192,160},{224,192},{256... | collective-permute-start | bytes 12296 | tf_op jit(solution)/shard_map/ppermute | solution.py:273
  10.9 0.8 %collective-permute-done.next_ref = f32[8,128]{1,0:T(8,128)S(1)} collective-permute-done((f32[8,128]{1,0:T(8,128)S(1)}, f32[8,128]{1,0:T(8,128)S(1)}, u32[]{:S(2)}, u32[]{:S(2)}) %collective-permute-start) | collective-permute-done | bytes 4128 | tf_op jit(solution)/shard_map/ppermute | solution.py:273
  11.8 0.1 shard_map.60
  11.8 15.9 %all_to_all.10 = f32[32,8,128]{2,1,0:T(8,128)S(1)} all-to-all(f32[32,8,128]{2,1,0:T(8,128)S(1)} %shard_map.60), channel_id=1, replica_groups=mesh['sub'=16,'tile'=32] {'tile'}, dimensions={0} | all-to-all | bytes 262144 | tf_op jit(solution)/shard_map/all_to_all | solution.py:274
  27.8 9.7 %shard_map.61 = (f32[2,8,128,256]{3,2,1,0:T(8,128)}, f32[8,8,8,128]{3,2,1,0:T(8,128)S(1)}, f32[8,8,8,128]{3,2,1,0:T(8,128)S(1)}) custom-call(s32[2]{0:T(128)S(1)} %pad_add_fusion.place_ref, f32[256,128]{1,0:T(8,128)S(1)} %bitcast.6), custom_call_target="tpu_custom_call" | custom-call | tf_op jit(solution)/shard_map/pallas_call | solution.py:249
  37.5 9.9 %collective-permute-start.1 = (f32[8,8,8,128]{3,2,1,0:T(8,128)S(1)}, f32[8,8,8,128]{3,2,1,0:T(8,128)S(1)}, u32[]{:S(2)}, u32[]{:S(2)}) collective-permute-start(f32[8,8,8,128]{3,2,1,0:T(8,128)S(1)} %get-tuple-element.7), channel_id=1, source_target_pairs={{0,32},{32,0},{64,96},{96,64},{128,160},{160,128},{192,224},{224,1... | collective-permute-start | bytes 786440 | tf_op jit(solution)/shard_map/ppermute | solution.py:276
  47.4 1.1 %collective-permute-done.1 = f32[8,8,8,128]{3,2,1,0:T(8,128)S(1)} collective-permute-done((f32[8,8,8,128]{3,2,1,0:T(8,128)S(1)}, f32[8,8,8,128]{3,2,1,0:T(8,128)S(1)}, u32[]{:S(2)}, u32[]{:S(2)}) %collective-permute-start.1) | collective-permute-done | bytes 262176 | tf_op jit(solution)/shard_map/ppermute | solution.py:276
  48.6 14.8 %all_to_all.11 = f32[8,8,8,128]{3,2,1,0:T(8,128)S(1)} all-to-all(f32[8,8,8,128]{3,2,1,0:T(8,128)S(1)} %max.3), channel_id=1, replica_groups={{0,64,128,192,256,320,384,448},{32,96,160,224,288,352,416,480},{1,65,12..., dimensions={0} | all-to-all | bytes 524288 | tf_op jit(solution)/shard_map/all_to_all | solution.py:279
  63.4 0.6 reduce_max.9
  (1 shorter events, 0.0 us)
Async XLA Ops:
  0.7 0.7 %copy-start = (f32[2,1,128]{2,1,0:T(1,128)S(1)}, f32[2,1,128]{2,1,0:T(1,128)}, u32[]{:S(2)}) copy-start(f32[2,1,128]{2,1,0:T(1,128)} %param.4) | copy-start | bytes 3076
  1.4 0.7 %copy-start.1 = (s32[2,1,64]{2,1,0:T(1,128)S(1)}, s32[2,1,64]{2,1,0:T(1,128)}, u32[]{:S(2)}) copy-start(s32[2,1,64]{2,1,0:T(1,128)} %param.6) | copy-start | bytes 1540
  2.1 0.7 %copy-start.2 = (s32[2,8]{1,0:T(2,128)S(1)}, s32[2,8]{1,0:T(2,128)}, u32[]{:S(2)}) copy-start(s32[2,8]{1,0:T(2,128)} %shown_ref.1) | copy-start | bytes 196
  2.7 0.7 %copy-start.3 = (f32[2,1]{0,1:T(1,128)S(1)}, f32[2,1]{0,1:T(1,128)}, u32[]{:S(2)}) copy-start(f32[2,1]{0,1:T(1,128)} %param.5) | copy-start | bytes 28
  4.1 7.7 %collective-permute-start = (f32[8,128]{1,0:T(8,128)S(1)}, f32[8,128]{1,0:T(8,128)S(1)}, u32[]{:S(2)}, u32[]{:S(2)}) collective-permute-start(f32[8,128]{1,0:T(8,128)S(1)} %shard_map.59.own_ref), channel_id=1, source_target_pairs={{32,0},{64,32},{96,64},{128,96},{160,128},{192,160},{224,192},{256... | collective-permute-start | bytes 12296 | tf_op jit(solution)/shard_map/ppermute | solution.py:273
  37.5 11.0 %collective-permute-start.1 = (f32[8,8,8,128]{3,2,1,0:T(8,128)S(1)}, f32[8,8,8,128]{3,2,1,0:T(8,128)S(1)}, u32[]{:S(2)}, u32[]{:S(2)}) collective-permute-start(f32[8,8,8,128]{3,2,1,0:T(8,128)S(1)} %get-tuple-element.7), channel_id=1, source_target_pairs={{0,32},{32,0},{64,96},{96,64},{128,160},{160,128},{192,224},{224,1... | collective-permute-start | bytes 786440 | tf_op jit(solution)/shard_map/ppermute | solution.py:276

commit v3 on v2

--- a/solution.py
+++ b/solution.py
@@ -69,7 +69,6 @@
         out_shape=jax.ShapeDtypeStruct((8, LANES), F32),
         in_specs=[pl.BlockSpec(memory_space=pltpu.SMEM)] + [vmem] * 4,
         out_specs=vmem,
-        compiler_params=pltpu.CompilerParams(vmem_limit_bytes=4 * 1024 * 1024),
     )(place, echoes, offset, gates, shown)
 
 
@@ -95,7 +94,7 @@
 
 
 def image_kernel(place_ref, g_ref, images_ref, keep_ref, send_ref,
-                 left_ref, right_ref, wave_ref, table_ref, prod_ref, out_ref, sems):
+                 left_a, left_b, right_a, right_b, wave_ref, table_ref, prod_ref, out_ref, power_ref, sems):
     tile_index = place_ref[0]
     core = place_ref[1] % 2
     x_first = ((tile_index % 2) * 1024 - 1024).astype(F32)
@@ -110,7 +109,7 @@
         t = pltpu.roll(m, FREQS, 1)
         return jnp.where(low, m[:16], t[16:]), jnp.where(low, t[:16], m[16:])
 
-    def build(half):
+    def tables(half):
         ca, sa = halved(2 * half)
         er, ei = halved(2 * half + 1)
         wave_ref[0:16, :] = ca
@@ -145,40 +144,50 @@
             phase = ca * (x_first + (255.5 + 512.0 * block)) + sa * (y_first + 63.5)
             put(16 + block, times((er * scale, ei * scale), sincos(phase)))
 
-        def chunk(c, carry):
-            def entry(slot):
-                return row(table_ref, slot * 32 + c), row(table_ref, slot * 32 + 16 + c)
-
-            w = sincos(row(wave_ref, c) * sigma)
-            for j in range(4):
-                a = times(w, entry(4 + j))
-                rows = [None] * 8
-                for m in range(4):
-                    rows[4 + m], rows[3 - m] = turned_both(a, entry(m))
-                for b in range(0, 8, 2):
+    def chunk(c, left_ref, right_ref):
+        def entry(slot):
+            return row(table_ref, slot * 32 + c), row(table_ref, slot * 32 + 16 + c)
+
+        w = sincos(row(wave_ref, c) * sigma)
+        for j in range(4):
+            a = times(w, entry(4 + j))
+            for m in (0, 2):
+                near, far = turned_both(a, entry(m)), turned_both(a, entry(m + 1))
+                for b, rows in ((4 + m, (near[0], far[0])), (2 - m, (far[1], near[1]))):
                     at = j * 64 + b * 8
                     for part in range(2):
                         left_ref[c, part * DEPTH + at: part * DEPTH + at + 16, :] = jnp.concatenate(
-                            [rows[b][part], rows[b + 1][part]], axis=0).astype(BF16)
-            v = sincos(row(wave_ref, 16 + c) * sigma)
-            for block in range(2):
-                a = times(v, entry(16 + block))
-                rows = [None] * 16
-                for m in range(8):
-                    rows[8 + m], rows[7 - m] = turned_both(a, entry(8 + m))
-                for b in range(0, 16, 2):
+                            [rows[0][part], rows[1][part]], axis=0).astype(BF16)
+        v = sincos(row(wave_ref, 16 + c) * sigma)
+        for block in range(2):
+            a = times(v, entry(16 + block))
+            for m in (0, 2, 4, 6):
+                near, far = turned_both(a, entry(8 + m)), turned_both(a, entry(9 + m))
+                for b, rows in ((8 + m, (near[0], far[0])), (6 - m, (far[1], near[1]))):
                     at = block * 256 + b * 8
                     for part in range(2):
                         right_ref[c, part * 128 + at: part * 128 + at + 16, :] = jnp.concatenate(
-                            [rows[b][part], rows[b + 1][part]], axis=0).astype(BF16)
-            return carry
-
-        lax.fori_loop(0, CHUNKS, chunk, 0)
-
-    def product(half):
-        left = jnp.concatenate([left_ref[c] for c in range(CHUNKS)], axis=1)
-        right = jnp.concatenate([right_ref[c] for c in range(CHUNKS)], axis=1)
-        prod_ref[half] = lax.dot_general(left, right, (((1,), (1,)), ((), ())), preferred_element_type=F32)
+                            [rows[0][part], rows[1][part]], axis=0).astype(BF16)
+
+    def product(left_ref, right_ref, rows, columns):
+        left = jnp.concatenate([left_ref[c, rows, :] for c in range(CHUNKS)], axis=1)
+        right = jnp.concatenate([right_ref[c, columns, :] for c in range(CHUNKS)], axis=1)
+        return lax.dot_general(left, right, (((1,), (1,)), ((), ())), preferred_element_type=F32)
+
+    def stage(done, made):
+        sides = ((left_a, right_a), (left_b, right_b))
+        tables(made)
+        if done is None:
+            lax.fori_loop(0, CHUNKS, lambda c, carry: (chunk(c, *sides[made % 2]), carry)[1], 0)
+        else:
+            def step(i, carry):
+                rows, columns = pl.ds(0, 512), pl.ds(pl.multiple_of(i * 256, 256), 256)
+                prod_ref[done, rows, columns] = product(*sides[done % 2], rows, columns)
+                for c in range(8):
+                    chunk(i * 8 + c, *sides[made % 2])
+                return carry
+
+            lax.fori_loop(0, 2, step, 0)
 
     def flip(v):
         return jnp.take_along_axis(v, backwards, axis=0)
@@ -191,53 +200,64 @@
     def out_copy(s, tile):
         return pltpu.make_async_copy(out_ref.at[s, tile], images_ref.at[s, tile], sems.at[s, tile])
 
-    for half in range(3):
-        build(half)
-        product(half)
-
-    for block in range(2):
+    def finish(s, block):
         for quarter in range(2):
             upper, lower = block * 4 + 2 + quarter, block * 4 + 1 - quarter
-            up = [weight(half, upper) for half in range(3)]
-            down = [weight(half, lower) for half in range(3)]
-
-            def finish(z, carry):
+            up = [weight(half, upper) for half in (s, s + 1)]
+            down = [weight(half, lower) for half in (s, s + 1)]
+            for z in range(8):
                 power_up, power_down = [], []
-                for c in range(2):
-                    r = 2 * z + c
-                    near = pl.ds(pl.multiple_of(quarter * 128 + r * 8, 8), 8)
-                    far = pl.ds(pl.multiple_of(DEPTH + quarter * 128 + r * 8, 8), 8)
+                for r in (2 * z, 2 * z + 1):
+                    near = slice(quarter * 128 + r * 8, quarter * 128 + r * 8 + 8)
+                    far = slice(DEPTH + near.start, DEPTH + near.stop)
                     above, below = [], []
-                    for half in range(3):
-                        pr = prod_ref[half, near, block * 256: block * 256 + 128]
-                        pi = prod_ref[half, near, block * 256 + 128: block * 256 + 256]
-                        qr = prod_ref[half, far, block * 256: block * 256 + 128]
-                        qi = prod_ref[half, far, block * 256 + 128: block * 256 + 256]
-                        above.append(((pr - qi) * up[half], (pi + qr) * up[half]))
-                        below.append(((pr + qi) * down[half], (pi - qr) * down[half]))
+                    for i in range(2):
+                        pr = prod_ref[s + i, near, block * 256: block * 256 + 128]
+                        pi = prod_ref[s + i, near, block * 256 + 128: block * 256 + 256]
+                        qr = prod_ref[s + i, far, block * 256: block * 256 + 128]
+                        qi = prod_ref[s + i, far, block * 256 + 128: block * 256 + 256]
+                        above.append(((pr - qi) * up[i], (pi + qr) * up[i]))
+                        below.append(((pr + qi) * down[i], (pi - qr) * down[i]))
                     for sums, tile, at, power, turn in ((above, upper, r, power_up, False),
                                                         (below, lower, 15 - r, power_down, True)):
-                        rows = pl.ds(pl.multiple_of(at * 8, 8), 8)
-                        most = None
-                        for s in range(2):
-                            re, im = (sums[s][part] + sums[s + 1][part] for part in range(2))
-                            if turn:
-                                re, im = flip(re), flip(im)
-                            out_ref[s, tile, rows, 0:128] = re
-                            out_ref[s, tile, rows, 128:256] = im
-                            now = re * re + im * im
-                            most = now if most is None else jnp.maximum(most, now)
-                        power.append(most)
-                keep_ref[z, upper] = jnp.where(core == 0, power_up[0], power_up[1])
-                send_ref[z, upper] = jnp.where(core == 0, power_up[1], power_up[0])
-                keep_ref[7 - z, lower] = jnp.where(core == 0, power_down[1], power_down[0])
-                send_ref[7 - z, lower] = jnp.where(core == 0, power_down[0], power_down[1])
-                return carry
-
-            lax.fori_loop(0, 8, finish, 0)
-            for s in range(2):
-                out_copy(s, upper).start()
-                out_copy(s, lower).start()
+                        rows = slice(at * 8, at * 8 + 8)
+                        re, im = (sums[0][part] + sums[1][part] for part in range(2))
+                        if turn:
+                            re, im = flip(re), flip(im)
+                        out_ref[s, tile, rows, 0:128] = re
+                        out_ref[s, tile, rows, 128:256] = im
+                        now = re * re + im * im
+                        if s == 0:
+                            power_ref[tile, rows, :] = now
+                        else:
+                            power.append(jnp.maximum(power_ref[tile, rows, :], now))
+                if s == 1:
+                    keep_ref[z, upper] = jnp.where(core == 0, power_up[0], power_up[1])
+                    send_ref[z, upper] = jnp.where(core == 0, power_up[1], power_up[0])
+                    keep_ref[7 - z, lower] = jnp.where(core == 0, power_down[1], power_down[0])
+                    send_ref[7 - z, lower] = jnp.where(core == 0, power_down[0], power_down[1])
+
+    def leave(s, block):
+        for tile in range(block * 4, block * 4 + 4):
+            out_copy(s, tile).start()
+
+    def last_product(block):
+        columns = slice(block * 256, block * 256 + 256)
+        prod_ref[2, :, columns] = product(left_a, right_a, slice(0, 2 * DEPTH), columns)
+
+    stage(None, 0)
+    stage(0, 1)
+    stage(1, 2)
+    last_product(0)
+    finish(0, 0)
+    finish(0, 1)
+    leave(0, 0)
+    leave(0, 1)
+    last_product(1)
+    finish(1, 0)
+    leave(1, 0)
+    finish(1, 1)
+    leave(1, 1)
     for s in range(2):
         for tile in range(TILES_DEV):
             out_copy(s, tile).wait()
@@ -253,11 +273,14 @@
         out_specs=(pl.BlockSpec(memory_space=pl.ANY), vmem, vmem),
         scratch_shapes=[
             pltpu.VMEM((CHUNKS, 2 * DEPTH, LANES), BF16),
+            pltpu.VMEM((CHUNKS, 2 * DEPTH, LANES), BF16),
+            pltpu.VMEM((CHUNKS, 512, LANES), BF16),
             pltpu.VMEM((CHUNKS, 512, LANES), BF16),
             pltpu.VMEM((32, LANES), F32),
             pltpu.VMEM((18 * 32, LANES), F32),
             pltpu.VMEM((3, 2 * DEPTH, 512), F32),
             pltpu.VMEM((2, TILES_DEV, PIX, 2 * PIX), F32),
+            pltpu.VMEM((TILES_DEV, PIX, PIX), F32),
             pltpu.SemaphoreType.DMA((2, TILES_DEV)),
         ],
         compiler_params=pltpu.CompilerParams(vmem_limit_bytes=40 * 1024 * 1024),

time: 64.3 us -> 63.1 us (0.981)
  local copies, waits for them, and re-layouts: 2.69 us -> 1.35 us
    pallas_call x1, Pallas kernels: 9.73 us -> 8.25 us  [image(): pl.pallas_call(image_kernel, out_shape=(jax.ShapeDtypeStruct((2, TILES_DE...]
    unnamed x8 -> x4, local copies, waits for them, and re-layouts: 2.69 us -> 1.35 us
    pallas_call x1, Pallas kernels: 0.7 us -> 1.55 us  [pack(): pl.pallas_call(pack_kernel, out_shape=jax.ShapeDtypeStruct((8, LANES), F3...]
where the time goes in v3:
time: 63.1 us; the launch traced here: 62.8 us
  blocking collectives  30.7 us (49%)
  starting transfers between devices  16.7 us (26%)
  Pallas kernels  9.88 us (16%)
  waiting for transfers between devices  2.17 us (3%)
  local copies, waits for them, and re-layouts  1.35 us (2%)
  other arithmetic  1.32 us (2%)
  between operations  0.66 us (1%)
    all_to_all x1, blocking collectives, on_device(): gathered = lax.all_to_all(spread(own, following), 'tile', 0, 0, tiled=True)  15.9 us
    all_to_all x1, blocking collectives, on_device(): lax.all_to_all(both, 'sub', 0, 0, tiled=True, axis_index_groups=groups)  14.8 us
    ppermute x1, starting transfers between devices, on_device(): other = lax.ppermute(send, 'sub', [(i, i ^ 1) for i in range(subs)])  9.87 us
    pallas_call x1, Pallas kernels, image(): pl.pallas_call(image_kernel, out_shape=(jax.ShapeDtypeStruct((2, TILES_DE...  8.25 us
    ppermute x1, starting transfers between devices, on_device(): lax.ppermute(own, 'sub', [((i + 1) % subs, i) for i in range(subs)])  6.84 us
    pallas_call x1, Pallas kernels, pack(): pl.pallas_call(pack_kernel, out_shape=jax.ShapeDtypeStruct((8, LANES), F3...  1.55 us
    unnamed x4, local copies, waits for them, and re-layouts  1.35 us
  transfers between devices with their start and end apart: 2, of which 2 were waited for; matrix products, arithmetic and copies ran while one was open for 0% of the time, Pallas kernels for 0%

profile of v3, /device:TPU:1, one launch (start us, length us, event | category | flops | bytes accessed | tf_op | source)
XLA Modules:
  0.0 62.8 jit_solution(13833113788268972490)
XLA Ops:
  0.6 0.6 %pad_add_fusion.place_ref = s32[2]{0:T(128)} fusion(s32[1]{0:T(128)} %bitcast.1, s32[1]{0:T(128)} %bitcast), kind=kLoop, calls=%fused_computation | loop fusion | flops 2 | bytes 16 | tf_op jit(solution)/shard_map/stack | solution.py:294
  1.3 1.6 %shard_map.59.own_ref = f32[8,128]{1,0:T(8,128)} custom-call(s32[2]{0:T(128)} %pad_add_fusion.place_ref, f32[2,128]{1,0:T(2,128)} %bitcast.7, f32[1,2]{1,0:T(1,128)} %bitcast.9, s32[2,64]{1,0:T(2,128)} %bitcast.8, s32[2,8]{1,0:T(2,128)} %shown_ref.1), custom_call_target="tpu_custom_call" | custom-call | tf_op jit(solution)/shard_map/pallas_call | solution.py:67
  2.8 6.8 %collective-permute-start = (f32[8,128]{1,0:T(8,128)}, f32[8,128]{1,0:T(8,128)S(1)}, u32[]{:S(2)}, u32[]{:S(2)}) collective-permute-start(f32[8,128]{1,0:T(8,128)} %shard_map.59.own_ref), channel_id=1, source_target_pairs={{32,0},{64,32},{96,64},{128,96},{160,128},{192,160},{224,192},{256... | collective-permute-start | bytes 12296 | tf_op jit(solution)/shard_map/ppermute | solution.py:296
  9.7 1.0 %collective-permute-done.next_ref = f32[8,128]{1,0:T(8,128)S(1)} collective-permute-done((f32[8,128]{1,0:T(8,128)}, f32[8,128]{1,0:T(8,128)S(1)}, u32[]{:S(2)}, u32[]{:S(2)}) %collective-permute-start) | collective-permute-done | bytes 4128 | tf_op jit(solution)/shard_map/ppermute | solution.py:296
  10.7 0.0 copy-start
  10.7 0.7 %copy-done = f32[8,128]{1,0:T(8,128)S(1)} copy-done((f32[8,128]{1,0:T(8,128)S(1)}, f32[8,128]{1,0:T(8,128)}, u32[]{:S(2)}) %copy-start) | copy-done | bytes 4120
  11.4 0.1 shard_map.60
  11.5 15.9 %all_to_all.10 = f32[32,8,128]{2,1,0:T(8,128)S(1)} all-to-all(f32[32,8,128]{2,1,0:T(8,128)S(1)} %shard_map.60), channel_id=1, replica_groups=mesh['sub'=16,'tile'=32] {'tile'}, dimensions={0} | all-to-all | bytes 262144 | tf_op jit(solution)/shard_map/all_to_all | solution.py:297
  27.4 0.0 copy-start.1
  27.4 0.7 %copy-done.1 = s32[2]{0:T(128)S(1)} copy-done((s32[2]{0:T(128)S(1)}, s32[2]{0:T(128)}, u32[]{:S(2)}) %copy-start.1) | copy-done | bytes 32
  28.1 8.2 %shard_map.61 = (f32[2,8,128,256]{3,2,1,0:T(8,128)}, f32[8,8,8,128]{3,2,1,0:T(8,128)S(1)}, f32[8,8,8,128]{3,2,1,0:T(8,128)S(1)}) custom-call(s32[2]{0:T(128)S(1)} %copy-done.1, f32[256,128]{1,0:T(8,128)S(1)} %bitcast.6), custom_call_target="tpu_custom_call" | custom-call | tf_op jit(solution)/shard_map/pallas_call | solution.py:269
  36.3 9.9 %collective-permute-start.1 = (f32[8,8,8,128]{3,2,1,0:T(8,128)S(1)}, f32[8,8,8,128]{3,2,1,0:T(8,128)S(1)}, u32[]{:S(2)}, u32[]{:S(2)}) collective-permute-start(f32[8,8,8,128]{3,2,1,0:T(8,128)S(1)} %get-tuple-element.7), channel_id=1, source_target_pairs={{0,32},{32,0},{64,96},{96,64},{128,160},{160,128},{192,224},{224,1... | collective-permute-start | bytes 786440 | tf_op jit(solution)/shard_map/ppermute | solution.py:299
  46.2 1.1 %collective-permute-done.1 = f32[8,8,8,128]{3,2,1,0:T(8,128)S(1)} collective-permute-done((f32[8,8,8,128]{3,2,1,0:T(8,128)S(1)}, f32[8,8,8,128]{3,2,1,0:T(8,128)S(1)}, u32[]{:S(2)}, u32[]{:S(2)}) %collective-permute-start.1) | collective-permute-done | bytes 262176 | tf_op jit(solution)/shard_map/ppermute | solution.py:299
  47.4 14.8 %all_to_all.11 = f32[8,8,8,128]{3,2,1,0:T(8,128)S(1)} all-to-all(f32[8,8,8,128]{3,2,1,0:T(8,128)S(1)} %max.3), channel_id=1, replica_groups={{0,64,128,192,256,320,384,448},{32,96,160,224,288,352,416,480},{1,65,12..., dimensions={0} | all-to-all | bytes 524288 | tf_op jit(solution)/shard_map/all_to_all | solution.py:302
  62.2 0.6 %reduce_max.9 = f32[8,8,128]{2,1,0:T(8,128)} reduce(f32[8,8,8,128]{3,2,1,0:T(8,128)S(1)} %all_to_all.11, f32[]{:T(128)} %constant.10.clone.1), dimensions={0}, to_apply=%region_0.0 | reduce | flops 57344 | bytes 294916 | tf_op jit(solution)/shard_map/reduce_max | solution.py:303
  (1 shorter events, 0.0 us)
Async XLA Ops:
  2.8 7.9 %collective-permute-start = (f32[8,128]{1,0:T(8,128)}, f32[8,128]{1,0:T(8,128)S(1)}, u32[]{:S(2)}, u32[]{:S(2)}) collective-permute-start(f32[8,128]{1,0:T(8,128)} %shard_map.59.own_ref), channel_id=1, source_target_pairs={{32,0},{64,32},{96,64},{128,96},{160,128},{192,160},{224,192},{256... | collective-permute-start | bytes 12296 | tf_op jit(solution)/shard_map/ppermute | solution.py:296
  10.7 0.7 %copy-start = (f32[8,128]{1,0:T(8,128)S(1)}, f32[8,128]{1,0:T(8,128)}, u32[]{:S(2)}) copy-start(f32[8,128]{1,0:T(8,128)} %shard_map.59.own_ref) | copy-start | bytes 12292
  27.4 0.7 %copy-start.1 = (s32[2]{0:T(128)S(1)}, s32[2]{0:T(128)}, u32[]{:S(2)}) copy-start(s32[2]{0:T(128)} %pad_add_fusion.place_ref) | copy-start | bytes 28
  36.3 11.0 %collective-permute-start.1 = (f32[8,8,8,128]{3,2,1,0:T(8,128)S(1)}, f32[8,8,8,128]{3,2,1,0:T(8,128)S(1)}, u32[]{:S(2)}, u32[]{:S(2)}) collective-permute-start(f32[8,8,8,128]{3,2,1,0:T(8,128)S(1)} %get-tuple-element.7), channel_id=1, source_target_pairs={{0,32},{32,0},{64,96},{96,64},{128,160},{160,128},{192,224},{224,1... | collective-permute-start | bytes 786440 | tf_op jit(solution)/shard_map/ppermute | solution.py:299

commit v4 on v3

--- a/solution.py
+++ b/solution.py
@@ -46,57 +46,56 @@
     return (p - q, r + t), (p + q, r - t)
 
 
-def pack_kernel(place_ref, echo_ref, offset_ref, gates_ref, shown_ref, out_ref):
+def pack_kernel(sub_ref, echo_hbm, offset_hbm, gates_hbm, shown_hbm, out_ref,
+                echo_ref, offset_ref, gates_ref, shown_ref, sems):
+    copies = [pltpu.make_async_copy(src, dst, sems.at[i]) for i, (src, dst) in enumerate((
+        (echo_hbm, echo_ref), (offset_hbm, offset_ref), (gates_hbm, gates_ref), (shown_hbm, shown_ref)))]
+    for copy in copies:
+        copy.start()
+    for copy in copies:
+        copy.wait()
     first = lax.broadcasted_iota(jnp.int32, (2, FREQS), 0)
-    half = (2 * place_ref[1] + first).astype(F32)
+    half = (2 * sub_ref[0] + first).astype(F32)
     offset = jnp.where(first == 0, offset_ref[0:1, 0:1], offset_ref[0:1, 1:2])
     angle = two_pi * (half + offset) / 32
     wave = 0.5 + gates_ref[...].astype(F32) / GATES
     cos, sin = sincos(angle)
     waves = jnp.concatenate([wave * cos, wave * sin], axis=1)
-    out_ref[...] = jnp.zeros_like(out_ref)
-    out_ref[0:1, :] = waves[0:1]
-    out_ref[1:2, :] = echo_ref[0:1, :]
-    out_ref[2:3, :] = waves[1:2]
-    out_ref[3:4, :] = echo_ref[1:2, :]
-    out_ref[4:6, 0:TILES_DEV] = shown_ref[...].astype(F32)
-
-
-def pack(place, echoes, offset, gates, shown):
+    at = lax.broadcasted_iota(jnp.int32, (8, LANES), 0)
+    tile = jnp.zeros((8, LANES), F32)
+    for i in range(2):
+        tile = jnp.where(at == 2 * i, waves[i:i + 1], tile)
+        tile = jnp.where(at == 2 * i + 1, echo_ref[i:i + 1, :], tile)
+    out_ref[...] = jnp.broadcast_to(tile[None], out_ref.shape)
+    shown = shown_ref[...].astype(F32)
+    out_ref[:, 4:6, 0:TILES_DEV] = jnp.broadcast_to(shown[None], (32, 2, TILES_DEV))
+
+
+def pack(sub, echoes, offset, gates, shown):
     vmem = pl.BlockSpec(memory_space=pltpu.VMEM)
     return pl.pallas_call(
         pack_kernel,
-        out_shape=jax.ShapeDtypeStruct((8, LANES), F32),
-        in_specs=[pl.BlockSpec(memory_space=pltpu.SMEM)] + [vmem] * 4,
+        out_shape=jax.ShapeDtypeStruct((32, 8, LANES), F32),
+        in_specs=[pl.BlockSpec(memory_space=pltpu.SMEM)] + [pl.BlockSpec(memory_space=pltpu.HBM)] * 4,
         out_specs=vmem,
-    )(place, echoes, offset, gates, shown)
-
-
-def spread_kernel(own_ref, next_ref, out_ref):
-    shown = jnp.concatenate([own_ref[4:5, 0:FREQS], own_ref[5:6, 0:FREQS]], axis=1)
-    tile = jnp.concatenate([own_ref[0:4, :], next_ref[0:2, :], shown, next_ref[4:5, :]], axis=0)
-    out_ref[...] = jnp.broadcast_to(tile[None], out_ref.shape)
-
-
-def spread(own, following):
-    vmem = pl.BlockSpec(memory_space=pltpu.VMEM)
-    return pl.pallas_call(
-        spread_kernel,
-        out_shape=jax.ShapeDtypeStruct((32, 8, LANES), F32),
-        in_specs=[vmem] * 2,
-        out_specs=vmem,
-        compiler_params=pltpu.CompilerParams(vmem_limit_bytes=4 * 1024 * 1024),
-    )(own, following)
+        scratch_shapes=[
+            pltpu.VMEM((2, LANES), F32),
+            pltpu.VMEM((1, 2), F32),
+            pltpu.VMEM((2, FREQS), jnp.int32),
+            pltpu.VMEM((2, TILES_DEV), jnp.int32),
+            pltpu.SemaphoreType.DMA((4,)),
+        ],
+    )(sub, echoes, offset, gates, shown)
 
 
 def row(ref, at):
     return jnp.broadcast_to(ref[pl.ds(at, 1), :], (8, LANES))
 
 
-def image_kernel(place_ref, g_ref, images_ref, keep_ref, send_ref,
+def image_kernel(tile_ref, sub_ref, g_ref, next_ref, images_ref, keep_ref, send_ref,
                  left_a, left_b, right_a, right_b, wave_ref, table_ref, prod_ref, out_ref, power_ref, sems):
-    tile_index = place_ref[0]
-    core = place_ref[1] % 2
+    tile_index = tile_ref[0]
+    core = sub_ref[0] % 2
     x_first = ((tile_index % 2) * 1024 - 1024).astype(F32)
     y_first = ((tile_index // 2) * 128 - 512).astype(F32)
     scale = F32((2.0 * PULSE_H * FREQS) ** -0.5)
@@ -104,14 +103,15 @@
     sigma = lax.broadcasted_iota(jnp.int32, (8, LANES), 0).astype(F32) - 3.5
     backwards = 7 - lax.broadcasted_iota(jnp.int32, (8, LANES), 0)
 
-    def halved(at):
-        m = g_ref[pl.ds(at, 32, stride=8), :]
+    def halved(ref, at):
+        m = ref[pl.ds(at, 32, stride=8), :]
         t = pltpu.roll(m, FREQS, 1)
         return jnp.where(low, m[:16], t[16:]), jnp.where(low, t[:16], m[16:])
 
     def tables(half):
-        ca, sa = halved(2 * half)
-        er, ei = halved(2 * half + 1)
+        ref, at = (g_ref, 2 * half) if half < 2 else (next_ref, 0)
+        ca, sa = halved(ref, at)
+        er, ei = halved(ref, at + 1)
         wave_ref[0:16, :] = ca
         wave_ref[16:32, :] = sa
 
@@ -193,9 +193,9 @@
         return jnp.take_along_axis(v, backwards, axis=0)
 
     def weight(half, tile):
-        lane = half * FREQS + tile if half < 2 else tile
-        own = g_ref[pl.ds(tile_index * 8 + (6 if half < 2 else 7), 1), :]
-        return jnp.broadcast_to(own[:, lane:lane + 1], (8, LANES))
+        ref, at = (g_ref, 4 + half) if half < 2 else (next_ref, 4)
+        own = ref[pl.ds(tile_index * 8 + at, 1), :]
+        return jnp.broadcast_to(own[:, tile:tile + 1], (8, LANES))
 
     def out_copy(s, tile):
         return pltpu.make_async_copy(out_ref.at[s, tile], images_ref.at[s, tile], sems.at[s, tile])
@@ -263,13 +263,13 @@
             out_copy(s, tile).wait()
 
 
-def image(place, gathered):
+def image(tile, sub, gathered, following):
     vmem = pl.BlockSpec(memory_space=pltpu.VMEM)
     piece = jax.ShapeDtypeStruct((8, TILES_DEV, 8, LANES), F32)
     return pl.pallas_call(
         image_kernel,
         out_shape=(jax.ShapeDtypeStruct((2, TILES_DEV, PIX, 2 * PIX), F32), piece, piece),
-        in_specs=[pl.BlockSpec(memory_space=pltpu.SMEM), vmem],
+        in_specs=[pl.BlockSpec(memory_space=pltpu.SMEM)] * 2 + [vmem] * 2,
         out_specs=(pl.BlockSpec(memory_space=pl.ANY), vmem, vmem),
         scratch_shapes=[
             pltpu.VMEM((CHUNKS, 2 * DEPTH, LANES), BF16),
@@ -284,18 +284,17 @@
             pltpu.SemaphoreType.DMA((2, TILES_DEV)),
         ],
         compiler_params=pltpu.CompilerParams(vmem_limit_bytes=40 * 1024 * 1024),
-    )(place, gathered)
+    )(tile, sub, gathered, following)
 
 
 def on_device(echoes, pulse_offset, range_gates, visible):
-    sub = lax.axis_index("sub")
-    tile = lax.axis_index("tile")
+    sub = lax.axis_index("sub").astype(jnp.int32)[None]
+    tile = lax.axis_index("tile").astype(jnp.int32)[None]
     subs = lax.axis_size("sub")
-    place = jnp.stack([tile, sub]).astype(jnp.int32)
-    own = pack(place, echoes[:, 0], pulse_offset.reshape(1, 2), range_gates[:, 0], visible)
-    following = lax.ppermute(own, "sub", [((i + 1) % subs, i) for i in range(subs)])
-    gathered = lax.all_to_all(spread(own, following), "tile", 0, 0, tiled=True)
-    images, keep, send = image(place, gathered.reshape(256, LANES))
+    own = pack(sub, echoes[:, 0], pulse_offset.reshape(1, 2), range_gates[:, 0], visible)
+    gathered = lax.all_to_all(own, "tile", 0, 0, tiled=True).reshape(256, LANES)
+    following = lax.ppermute(gathered, "sub", [((i + 1) % subs, i) for i in range(subs)])
+    images, keep, send = image(tile, sub, gathered, following)
     other = lax.ppermute(send, "sub", [(i, i ^ 1) for i in range(subs)])
     both = jnp.maximum(keep, other)
     groups = [[2 * z + c for z in range(subs // 2)] for c in range(2)]

time: 63.1 us -> 62 us (0.983)
  starting transfers between devices: 16.7 us -> 8.95 us
  blocking collectives: 30.7 us -> 36.4 us
  waiting for transfers between devices: 2.17 us -> 5.77 us
  local copies, waits for them, and re-layouts: 1.35 us -> 0 us
  other arithmetic: 1.32 us -> 0.67 us
    ppermute x1, starting transfers between devices: 6.84 us -> 2.06 us  [on_device(): lax.ppermute(gathered, 'sub', [((i + 1) % subs, i) for i in range(subs)])]
    all_to_all x1, blocking collectives: 15.9 us -> 19.8 us  [on_device(): gathered = lax.all_to_all(own, 'tile', 0, 0, tiled=True).reshape(256, LANES)]
    ppermute x1, waiting for transfers between devices: 1.03 us -> 4.63 us  [on_device(): lax.ppermute(gathered, 'sub', [((i + 1) % subs, i) for i in range(subs)])]
    ppermute x1, starting transfers between devices: 9.87 us -> 6.89 us  [on_device(): other = lax.ppermute(send, 'sub', [(i, i ^ 1) for i in range(subs)])]
    all_to_all x1, blocking collectives: 14.8 us -> 16.6 us  [on_device(): lax.all_to_all(both, 'sub', 0, 0, tiled=True, axis_index_groups=groups)]
    unnamed x4 -> x0, local copies, waits for them, and re-layouts: 1.35 us -> none
    another operation x1 -> x0, other arithmetic: 0.65 us -> none  [on_device(): place = jnp.stack([tile, sub]).astype(jnp.int32)]
    pallas_call x2 -> x1, Pallas kernels: 1.63 us -> 1.59 us  [pack(): pl.pallas_call(pack_kernel, out_shape=jax.ShapeDtypeStruct((32, 8, LANES)...]
where the time goes in v4:
time: 62 us; the launch traced here: 61.8 us
  blocking collectives  36.4 us (59%)
  Pallas kernels  9.3 us (15%)
  starting transfers between devices  8.95 us (14%)
  waiting for transfers between devices  5.77 us (9%)
  other arithmetic  0.67 us (1%)
  between operations  0.66 us (1%)
    all_to_all x1, blocking collectives, on_device(): gathered = lax.all_to_all(own, 'tile', 0, 0, tiled=True).reshape(256, LANES)  19.8 us
    all_to_all x1, blocking collectives, on_device(): lax.all_to_all(both, 'sub', 0, 0, tiled=True, axis_index_groups=groups)  16.6 us
    pallas_call x1, Pallas kernels, image(): pl.pallas_call(image_kernel, out_shape=(jax.ShapeDtypeStruct((2, TILES_DE...  7.7 us
    ppermute x1, starting transfers between devices, on_device(): other = lax.ppermute(send, 'sub', [(i, i ^ 1) for i in range(subs)])  6.89 us
    ppermute x1, waiting for transfers between devices, on_device(): lax.ppermute(gathered, 'sub', [((i + 1) % subs, i) for i in range(subs)])  4.63 us
    ppermute x1, starting transfers between devices, on_device(): lax.ppermute(gathered, 'sub', [((i + 1) % subs, i) for i in range(subs)])  2.06 us
    pallas_call x1, Pallas kernels, pack(): pl.pallas_call(pack_kernel, out_shape=jax.ShapeDtypeStruct((32, 8, LANES)...  1.59 us
  transfers between devices with their start and end apart: 2, of which 2 were waited for; matrix products, arithmetic and copies ran while one was open for 0% of the time, Pallas kernels for 0%

profile of v4, /device:TPU:1, one launch (start us, length us, event | category | flops | bytes accessed | tf_op | source)
XLA Modules:
  0.0 61.8 jit_solution(2404809963151929494)
XLA Ops:
  0.6 1.6 %shard_map.59 = f32[32,8,128]{2,1,0:T(8,128)} custom-call(s32[1]{0:T(128)} %bitcast.1.sub_ref, f32[2,128]{1,0:T(2,128)} %bitcast.8, f32[1,2]{1,0:T(1,128)} %bitcast.10, s32[2,64]{1,0:T(2,128)} %bitcast.9, s32[2,8]{1,0:T(2,128)} %shown_hbm.1), custom_call_target="tpu_custom_call" | custom-call | tf_op jit(solution)/shard_map/pallas_call | solution.py:76
  2.2 19.8 %all_to_all.10 = f32[32,8,128]{2,1,0:T(8,128)S(1)} all-to-all(f32[32,8,128]{2,1,0:T(8,128)} %shard_map.59), channel_id=1, replica_groups=mesh['sub'=16,'tile'=32] {'tile'}, dimensions={0} | all-to-all | bytes 262144 | tf_op jit(solution)/shard_map/all_to_all | solution.py:295
  22.1 2.1 %collective-permute-start = (f32[256,128]{1,0:T(8,128)S(1)}, f32[256,128]{1,0:T(8,128)S(1)}, u32[]{:S(2)}, u32[]{:S(2)}) collective-permute-start(f32[256,128]{1,0:T(8,128)S(1)} %bitcast.6), channel_id=1, source_target_pairs={{32,0},{64,32},{96,64},{128,96},{160,128},{192,160},{224,192},{256... | collective-permute-start | bytes 393224 | tf_op jit(solution)/shard_map/ppermute | solution.py:296
  24.1 4.6 %collective-permute-done.next_ref = f32[256,128]{1,0:T(8,128)S(1)} collective-permute-done((f32[256,128]{1,0:T(8,128)S(1)}, f32[256,128]{1,0:T(8,128)S(1)}, u32[]{:S(2)}, u32[]{:S(2)}) %collective-permute-start) | collective-permute-done | bytes 131104 | tf_op jit(solution)/shard_map/ppermute | solution.py:296
  28.8 7.7 %shard_map.60 = (f32[2,8,128,256]{3,2,1,0:T(8,128)}, f32[8,8,8,128]{3,2,1,0:T(8,128)S(1)}, f32[8,8,8,128]{3,2,1,0:T(8,128)S(1)}) custom-call(s32[1]{0:T(128)} %bitcast.tile_ref, s32[1]{0:T(128)} %bitcast.1.sub_ref, f32[256,128]{1,0:T(8,128)S(1)} %bitcast.7, f32[256,128]{1,0:T(8,128)S(1)} %collective-permute-done.next_ref), custom_call_target="tpu_custom_call" | custom-call | tf_op jit(solution)/shard_map/pallas_call | solution.py:269
  36.5 6.9 %collective-permute-start.1 = (f32[8,8,8,128]{3,2,1,0:T(8,128)S(1)}, f32[8,8,8,128]{3,2,1,0:T(8,128)S(1)}, u32[]{:S(2)}, u32[]{:S(2)}) collective-permute-start(f32[8,8,8,128]{3,2,1,0:T(8,128)S(1)} %get-tuple-element.7), channel_id=1, source_target_pairs={{0,32},{32,0},{64,96},{96,64},{128,160},{160,128},{192,224},{224,1... | collective-permute-start | bytes 786440 | tf_op jit(solution)/shard_map/ppermute | solution.py:298
  43.4 1.1 %collective-permute-done.1 = f32[8,8,8,128]{3,2,1,0:T(8,128)S(1)} collective-permute-done((f32[8,8,8,128]{3,2,1,0:T(8,128)S(1)}, f32[8,8,8,128]{3,2,1,0:T(8,128)S(1)}, u32[]{:S(2)}, u32[]{:S(2)}) %collective-permute-start.1) | collective-permute-done | bytes 262176 | tf_op jit(solution)/shard_map/ppermute | solution.py:298
  44.6 16.6 %all_to_all.11 = f32[8,8,8,128]{3,2,1,0:T(8,128)S(1)} all-to-all(f32[8,8,8,128]{3,2,1,0:T(8,128)S(1)} %max.3), channel_id=1, replica_groups={{0,64,128,192,256,320,384,448},{32,96,160,224,288,352,416,480},{1,65,12..., dimensions={0} | all-to-all | bytes 524288 | tf_op jit(solution)/shard_map/all_to_all | solution.py:301
  61.1 0.6 %reduce_max.9 = f32[8,8,128]{2,1,0:T(8,128)} reduce(f32[8,8,8,128]{3,2,1,0:T(8,128)S(1)} %all_to_all.11, f32[]{:T(128)} %constant.10.clone.1), dimensions={0}, to_apply=%region_0.0 | reduce | flops 57344 | bytes 294916 | tf_op jit(solution)/shard_map/reduce_max | solution.py:302
  (1 shorter events, 0.0 us)
Async XLA Ops:
  22.1 6.7 %collective-permute-start = (f32[256,128]{1,0:T(8,128)S(1)}, f32[256,128]{1,0:T(8,128)S(1)}, u32[]{:S(2)}, u32[]{:S(2)}) collective-permute-start(f32[256,128]{1,0:T(8,128)S(1)} %bitcast.6), channel_id=1, source_target_pairs={{32,0},{64,32},{96,64},{128,96},{160,128},{192,160},{224,192},{256... | collective-permute-start | bytes 393224 | tf_op jit(solution)/shard_map/ppermute | solution.py:296
  36.5 8.0 %collective-permute-start.1 = (f32[8,8,8,128]{3,2,1,0:T(8,128)S(1)}, f32[8,8,8,128]{3,2,1,0:T(8,128)S(1)}, u32[]{:S(2)}, u32[]{:S(2)}) collective-permute-start(f32[8,8,8,128]{3,2,1,0:T(8,128)S(1)} %get-tuple-element.7), channel_id=1, source_target_pairs={{0,32},{32,0},{64,96},{96,64},{128,160},{160,128},{192,224},{224,1... | collective-permute-start | bytes 786440 | tf_op jit(solution)/shard_map/ppermute | solution.py:298

commit v5 on v4

--- a/solution.py
+++ b/solution.py
@@ -92,10 +92,10 @@
     return jnp.broadcast_to(ref[pl.ds(at, 1), :], (8, LANES))
 
 
-def image_kernel(tile_ref, sub_ref, g_ref, next_ref, images_ref, keep_ref, send_ref,
-                 left_a, left_b, right_a, right_b, wave_ref, table_ref, prod_ref, out_ref, power_ref, sems):
+def steps(tile_ref, sub_ref, g_ref, next_ref, sides, wave_ref, table_ref, prods, images_ref, out_ref, power_ref, sems,
+          keep_ref=None, send_ref=None):
     tile_index = tile_ref[0]
-    core = sub_ref[0] % 2
+    core = sub_ref[0] % 2 if sub_ref is not None else None
     x_first = ((tile_index % 2) * 1024 - 1024).astype(F32)
     y_first = ((tile_index // 2) * 128 - 512).astype(F32)
     scale = F32((2.0 * PULSE_H * FREQS) ** -0.5)
@@ -175,14 +175,13 @@
         return lax.dot_general(left, right, (((1,), (1,)), ((), ())), preferred_element_type=F32)
 
     def stage(done, made):
-        sides = ((left_a, right_a), (left_b, right_b))
         tables(made)
         if done is None:
             lax.fori_loop(0, CHUNKS, lambda c, carry: (chunk(c, *sides[made % 2]), carry)[1], 0)
         else:
             def step(i, carry):
                 rows, columns = pl.ds(0, 512), pl.ds(pl.multiple_of(i * 256, 256), 256)
-                prod_ref[done, rows, columns] = product(*sides[done % 2], rows, columns)
+                prods[done][rows, columns] = product(*sides[done % 2], rows, columns)
                 for c in range(8):
                     chunk(i * 8 + c, *sides[made % 2])
                 return carry
@@ -198,7 +197,7 @@
         return jnp.broadcast_to(own[:, tile:tile + 1], (8, LANES))
 
     def out_copy(s, tile):
-        return pltpu.make_async_copy(out_ref.at[s, tile], images_ref.at[s, tile], sems.at[s, tile])
+        return pltpu.make_async_copy(out_ref.at[tile], images_ref.at[s, tile], sems.at[tile])
 
     def finish(s, block):
         for quarter in range(2):
@@ -212,10 +211,10 @@
                     far = slice(DEPTH + near.start, DEPTH + near.stop)
                     above, below = [], []
                     for i in range(2):
-                        pr = prod_ref[s + i, near, block * 256: block * 256 + 128]
-                        pi = prod_ref[s + i, near, block * 256 + 128: block * 256 + 256]
-                        qr = prod_ref[s + i, far, block * 256: block * 256 + 128]
-                        qi = prod_ref[s + i, far, block * 256 + 128: block * 256 + 256]
+                        pr = prods[s + i][near, block * 256: block * 256 + 128]
+                        pi = prods[s + i][near, block * 256 + 128: block * 256 + 256]
+                        qr = prods[s + i][far, block * 256: block * 256 + 128]
+                        qi = prods[s + i][far, block * 256 + 128: block * 256 + 256]
                         above.append(((pr - qi) * up[i], (pi + qr) * up[i]))
                         below.append(((pr + qi) * down[i], (pi - qr) * down[i]))
                     for sums, tile, at, power, turn in ((above, upper, r, power_up, False),
@@ -224,8 +223,8 @@
                         re, im = (sums[0][part] + sums[1][part] for part in range(2))
                         if turn:
                             re, im = flip(re), flip(im)
-                        out_ref[s, tile, rows, 0:128] = re
-                        out_ref[s, tile, rows, 128:256] = im
+                        out_ref[tile, rows, 0:128] = re
+                        out_ref[tile, rows, 128:256] = im
                         now = re * re + im * im
                         if s == 0:
                             power_ref[tile, rows, :] = now
@@ -241,50 +240,85 @@
         for tile in range(block * 4, block * 4 + 4):
             out_copy(s, tile).start()
 
-    def last_product(block):
+    def last_product(half, block):
         columns = slice(block * 256, block * 256 + 256)
-        prod_ref[2, :, columns] = product(left_a, right_a, slice(0, 2 * DEPTH), columns)
-
+        prods[half][:, columns] = product(*sides[half % 2], slice(0, 2 * DEPTH), columns)
+
+    return stage, last_product, finish, leave, out_copy
+
+
+def first_kernel(tile_ref, g_ref, images_ref, second_ref, power_ref,
+                 left_a, left_b, right_a, right_b, wave_ref, table_ref, prod_ref, out_ref, sems):
+    stage, last_product, finish, leave, out_copy = steps(
+        tile_ref, None, g_ref, None, ((left_a, right_a), (left_b, right_b)), wave_ref, table_ref,
+        (prod_ref, second_ref), images_ref, out_ref, power_ref, sems)
     stage(None, 0)
     stage(0, 1)
-    stage(1, 2)
-    last_product(0)
+    last_product(1, 0)
+    last_product(1, 1)
     finish(0, 0)
+    leave(0, 0)
     finish(0, 1)
-    leave(0, 0)
     leave(0, 1)
-    last_product(1)
+    for tile in range(TILES_DEV):
+        out_copy(0, tile).wait()
+
+
+def second_kernel(tile_ref, sub_ref, g_ref, next_ref, second_ref, power_ref, before_ref, images_ref, keep_ref, send_ref,
+                  left_ref, right_ref, wave_ref, table_ref, prod_ref, out_ref, sems):
+    stage, last_product, finish, leave, out_copy = steps(
+        tile_ref, sub_ref, g_ref, next_ref, ((left_ref, right_ref),), wave_ref, table_ref,
+        (None, second_ref, prod_ref), images_ref, out_ref, power_ref, sems, keep_ref, send_ref)
+    stage(None, 2)
+    last_product(2, 0)
+    last_product(2, 1)
     finish(1, 0)
     leave(1, 0)
     finish(1, 1)
     leave(1, 1)
-    for s in range(2):
-        for tile in range(TILES_DEV):
-            out_copy(s, tile).wait()
-
-
-def image(tile, sub, gathered, following):
-    vmem = pl.BlockSpec(memory_space=pltpu.VMEM)
+    for tile in range(TILES_DEV):
+        out_copy(1, tile).wait()
+
+
+def scratch(sides):
+    return [
+        *[pltpu.VMEM((CHUNKS, 2 * DEPTH, LANES), BF16)] * sides,
+        *[pltpu.VMEM((CHUNKS, 512, LANES), BF16)] * sides,
+        pltpu.VMEM((32, LANES), F32),
+        pltpu.VMEM((18 * 32, LANES), F32),
+        pltpu.VMEM((2 * DEPTH, 512), F32),
+        pltpu.VMEM((TILES_DEV, PIX, 2 * PIX), F32),
+        pltpu.SemaphoreType.DMA((TILES_DEV,)),
+    ]
+
+
+def first(tile, gathered):
+    vmem, smem, anywhere = (pl.BlockSpec(memory_space=space) for space in (pltpu.VMEM, pltpu.SMEM, pl.ANY))
+    return pl.pallas_call(
+        first_kernel,
+        out_shape=(jax.ShapeDtypeStruct((2, TILES_DEV, PIX, 2 * PIX), F32),
+                   jax.ShapeDtypeStruct((2 * DEPTH, 512), F32),
+                   jax.ShapeDtypeStruct((TILES_DEV, PIX, PIX), F32)),
+        in_specs=[smem, vmem],
+        out_specs=(anywhere, vmem, vmem),
+        scratch_shapes=scratch(2),
+        cost_estimate=pl.CostEstimate(flops=2 * 2 * 512 * 512 * 2048, bytes_accessed=8 << 20, transcendentals=0),
+        compiler_params=pltpu.CompilerParams(vmem_limit_bytes=32 * 1024 * 1024),
+    )(tile, gathered)
+
+
+def second(tile, sub, gathered, following, product, power, images):
+    vmem, smem, anywhere = (pl.BlockSpec(memory_space=space) for space in (pltpu.VMEM, pltpu.SMEM, pl.ANY))
     piece = jax.ShapeDtypeStruct((8, TILES_DEV, 8, LANES), F32)
     return pl.pallas_call(
-        image_kernel,
+        second_kernel,
         out_shape=(jax.ShapeDtypeStruct((2, TILES_DEV, PIX, 2 * PIX), F32), piece, piece),
-        in_specs=[pl.BlockSpec(memory_space=pltpu.SMEM)] * 2 + [vmem] * 2,
-        out_specs=(pl.BlockSpec(memory_space=pl.ANY), vmem, vmem),
-        scratch_shapes=[
-            pltpu.VMEM((CHUNKS, 2 * DEPTH, LANES), BF16),
-            pltpu.VMEM((CHUNKS, 2 * DEPTH, LANES), BF16),
-            pltpu.VMEM((CHUNKS, 512, LANES), BF16),
-            pltpu.VMEM((CHUNKS, 512, LANES), BF16),
-            pltpu.VMEM((32, LANES), F32),
-            pltpu.VMEM((18 * 32, LANES), F32),
-            pltpu.VMEM((3, 2 * DEPTH, 512), F32),
-            pltpu.VMEM((2, TILES_DEV, PIX, 2 * PIX), F32),
-            pltpu.VMEM((TILES_DEV, PIX, PIX), F32),
-            pltpu.SemaphoreType.DMA((2, TILES_DEV)),
-        ],
-        compiler_params=pltpu.CompilerParams(vmem_limit_bytes=40 * 1024 * 1024),
-    )(tile, sub, gathered, following)
+        in_specs=[smem, smem, vmem, vmem, vmem, vmem, anywhere],
+        out_specs=(anywhere, vmem, vmem),
+        scratch_shapes=scratch(1),
+        input_output_aliases={6: 0},
+        compiler_params=pltpu.CompilerParams(vmem_limit_bytes=32 * 1024 * 1024),
+    )(tile, sub, gathered, following, product, power, images)
 
 
 def on_device(echoes, pulse_offset, range_gates, visible):
@@ -294,7 +328,8 @@
     own = pack(sub, echoes[:, 0], pulse_offset.reshape(1, 2), range_gates[:, 0], visible)
     gathered = lax.all_to_all(own, "tile", 0, 0, tiled=True).reshape(256, LANES)
     following = lax.ppermute(gathered, "sub", [((i + 1) % subs, i) for i in range(subs)])
-    images, keep, send = image(tile, sub, gathered, following)
+    images, product, power = first(tile, gathered)
+    images, keep, send = second(tile, sub, gathered, following, product, power, images)
     other = lax.ppermute(send, "sub", [(i, i ^ 1) for i in range(subs)])
     both = jnp.maximum(keep, other)
     groups = [[2 * z + c for z in range(subs // 2)] for c in range(2)]

time: 62 us -> 60 us (0.968)
  blocking collectives: 36.4 us -> 15.4 us
  starting transfers between devices: 8.95 us -> 21.6 us
  waiting for transfers between devices: 5.77 us -> 10.5 us
  Pallas kernels: 9.3 us -> 10.9 us
    all_to_all x1 -> x0, blocking collectives: 19.8 us -> none  [on_device(): gathered = lax.all_to_all(own, 'tile', 0, 0, tiled=True).reshape(256, LANES)]
    all_to_all x0 -> x1, starting transfers between devices: none -> 10.5 us  [on_device(): gathered = lax.all_to_all(own, 'tile', 0, 0, tiled=True).reshape(256, LANES)]
    all_to_all x0 -> x1, waiting for transfers between devices: none -> 9.35 us  [on_device(): gathered = lax.all_to_all(own, 'tile', 0, 0, tiled=True).reshape(256, LANES)]
    ppermute x1, waiting for transfers between devices: 4.63 us -> 0.01 us  [on_device(): lax.ppermute(gathered, 'sub', [((i + 1) % subs, i) for i in range(subs)])]
    ppermute x1, starting transfers between devices: 6.89 us -> 9 us  [on_device(): other = lax.ppermute(send, 'sub', [(i, i ^ 1) for i in range(subs)])]
    pallas_call x1 -> x2, Pallas kernels: 7.7 us -> 9.33 us  [the longest x1 5.56 us: first(): pl.pallas_call(first_kernel, out_shape=(jax.ShapeDtypeStruct((2, TILES_DE...]
    all_to_all x1, blocking collectives: 16.6 us -> 15.4 us  [on_device(): lax.all_to_all(both, 'sub', 0, 0, tiled=True, axis_index_groups=groups)]
  transfers between devices with their start and end apart: 2 -> 3, of which waited for: 2 -> 2; matrix products, arithmetic and copies ran while one was open for 0% -> 0% of each run, Pallas kernels for 0% -> 9%
where the time goes in v5:
time: 60 us; the launch traced here: 59.7 us
  starting transfers between devices  21.6 us (36%)
  blocking collectives  15.4 us (26%)
  Pallas kernels  10.9 us (18%)
  waiting for transfers between devices  10.5 us (18%)
  between operations  0.69 us (1%)
  other arithmetic  0.67 us (1%)
    all_to_all x1, blocking collectives, on_device(): lax.all_to_all(both, 'sub', 0, 0, tiled=True, axis_index_groups=groups)  15.4 us
    all_to_all x1, starting transfers between devices, on_device(): gathered = lax.all_to_all(own, 'tile', 0, 0, tiled=True).reshape(256, LANES)  10.5 us
    all_to_all x1, waiting for transfers between devices, on_device(): gathered = lax.all_to_all(own, 'tile', 0, 0, tiled=True).reshape(256, LANES)  9.35 us
    ppermute x1, starting transfers between devices, on_device(): other = lax.ppermute(send, 'sub', [(i, i ^ 1) for i in range(subs)])  9 us
    pallas_call x1, Pallas kernels, first(): pl.pallas_call(first_kernel, out_shape=(jax.ShapeDtypeStruct((2, TILES_DE...  5.56 us
    pallas_call x1, Pallas kernels, second(): pl.pallas_call(second_kernel, out_shape=(jax.ShapeDtypeStruct((2, TILES_D...  3.77 us
    ppermute x1, starting transfers between devices, on_device(): lax.ppermute(gathered, 'sub', [((i + 1) % subs, i) for i in range(subs)])  2.06 us
    pallas_call x1, Pallas kernels, pack(): pl.pallas_call(pack_kernel, out_shape=jax.ShapeDtypeStruct((32, 8, LANES)...  1.59 us
  transfers between devices with their start and end apart: 3, of which 2 were waited for; matrix products, arithmetic and copies ran while one was open for 0% of the time, Pallas kernels for 9%

profile of v5, /device:TPU:1, one launch (start us, length us, event | category | flops | bytes accessed | tf_op | source)
XLA Modules:
  0.0 59.7 jit_solution(6969458998977739258)
XLA Ops:
  0.6 1.6 %shard_map.59 = f32[32,8,128]{2,1,0:T(8,128)} custom-call(s32[1]{0:T(128)} %bitcast.1.sub_ref, f32[2,128]{1,0:T(2,128)} %bitcast.9, f32[1,2]{1,0:T(1,128)} %bitcast.11, s32[2,64]{1,0:T(2,128)} %bitcast.10, s32[2,8]{1,0:T(2,128)} %shown_hbm.1), custom_call_target="tpu_custom_call" | custom-call | tf_op jit(solution)/shard_map/pallas_call | solution.py:76
  2.2 10.5 %all-to-all-start = ((f32[32,8,128]{2,1,0:T(8,128)}), f32[32,8,128]{2,1,0:T(8,128)S(1)}, u32[]{:S(2)}, u32[]{:S(2)}) async-start(f32[32,8,128]{2,1,0:T(8,128)} %shard_map.59), calls=%async_computation | async-start | bytes 262144 | tf_op jit(solution)/shard_map/all_to_all | solution.py:329
  12.7 9.3 %all-to-all-done = f32[32,8,128]{2,1,0:T(8,128)S(1)} async-done(((f32[32,8,128]{2,1,0:T(8,128)}), f32[32,8,128]{2,1,0:T(8,128)S(1)}, u32[]{:S(2)}, u32[]{:S(2)}) %all-to-all-start) | async-done | bytes 131104 | tf_op jit(solution)/shard_map/all_to_all | solution.py:329
  22.1 2.1 %collective-permute-start = (f32[256,128]{1,0:T(8,128)S(1)}, f32[256,128]{1,0:T(8,128)S(1)}, u32[]{:S(2)}, u32[]{:S(2)}) collective-permute-start(f32[256,128]{1,0:T(8,128)S(1)} %bitcast.6), channel_id=1, source_target_pairs={{32,0},{64,32},{96,64},{128,96},{160,128},{192,160},{224,192},{256... | collective-permute-start | bytes 393224 | tf_op jit(solution)/shard_map/ppermute | solution.py:330
  24.2 5.6 %shard_map.60 = (f32[2,8,128,256]{3,2,1,0:T(8,128)}, f32[512,512]{1,0:T(8,128)S(1)}, f32[8,128,128]{2,1,0:T(8,128)S(1)}) custom-call(s32[1]{0:T(128)} %bitcast.tile_ref, f32[256,128]{1,0:T(8,128)S(1)} %bitcast.7), custom_call_target="tpu_custom_call" | custom-call | flops 2147483648 | bytes 8388608 | tf_op jit(solution)/shard_map/pallas_call | solution.py:297
  29.7 0.0 collective-permute-done.next_ref
  29.7 3.8 %shard_map.61 = (f32[2,8,128,256]{3,2,1,0:T(8,128)}, f32[8,8,8,128]{3,2,1,0:T(8,128)S(1)}, f32[8,8,8,128]{3,2,1,0:T(8,128)S(1)}) custom-call(s32[1]{0:T(128)} %bitcast.tile_ref, s32[1]{0:T(128)} %bitcast.1.sub_ref, f32[256,128]{1,0:T(8,128)S(1)} %bitcast.8, f32[256,128]{1,0:T(8,128)S(1)} %collective-permute-done.next_ref, ...), custom_call_target="tpu_custom_call", output_to_operand_aliasing={{0}: (6, {})} | custom-call | tf_op jit(solution)/shard_map/pallas_call | solution.py:313
  33.5 9.0 %collective-permute-start.1 = (f32[8,8,8,128]{3,2,1,0:T(8,128)S(1)}, f32[8,8,8,128]{3,2,1,0:T(8,128)S(1)}, u32[]{:S(2)}, u32[]{:S(2)}) collective-permute-start(f32[8,8,8,128]{3,2,1,0:T(8,128)S(1)} %get-tuple-element.13), channel_id=1, source_target_pairs={{0,32},{32,0},{64,96},{96,64},{128,160},{160,128},{192,224},{224,1... | collective-permute-start | bytes 786440 | tf_op jit(solution)/shard_map/ppermute | solution.py:333
  42.5 1.1 %collective-permute-done.1 = f32[8,8,8,128]{3,2,1,0:T(8,128)S(1)} collective-permute-done((f32[8,8,8,128]{3,2,1,0:T(8,128)S(1)}, f32[8,8,8,128]{3,2,1,0:T(8,128)S(1)}, u32[]{:S(2)}, u32[]{:S(2)}) %collective-permute-start.1) | collective-permute-done | bytes 262176 | tf_op jit(solution)/shard_map/ppermute | solution.py:333
  43.7 15.4 %all_to_all.10 = f32[8,8,8,128]{3,2,1,0:T(8,128)S(1)} all-to-all(f32[8,8,8,128]{3,2,1,0:T(8,128)S(1)} %max.3), channel_id=1, replica_groups={{0,64,128,192,256,320,384,448},{32,96,160,224,288,352,416,480},{1,65,12..., dimensions={0} | all-to-all | bytes 524288 | tf_op jit(solution)/shard_map/all_to_all | solution.py:336
  59.1 0.6 %reduce_max.9 = f32[8,8,128]{2,1,0:T(8,128)} reduce(f32[8,8,8,128]{3,2,1,0:T(8,128)S(1)} %all_to_all.10, f32[]{:T(128)} %constant.10.clone.1), dimensions={0}, to_apply=%region_0.0 | reduce | flops 57344 | bytes 294916 | tf_op jit(solution)/shard_map/reduce_max | solution.py:337
  (1 shorter events, 0.0 us)
Async XLA Ops:
  2.2 19.9 %all-to-all-start = ((f32[32,8,128]{2,1,0:T(8,128)}), f32[32,8,128]{2,1,0:T(8,128)S(1)}, u32[]{:S(2)}, u32[]{:S(2)}) async-start(f32[32,8,128]{2,1,0:T(8,128)} %shard_map.59), calls=%async_computation | async-start | bytes 262144 | tf_op jit(solution)/shard_map/all_to_all | solution.py:329
  22.1 7.6 %collective-permute-start = (f32[256,128]{1,0:T(8,128)S(1)}, f32[256,128]{1,0:T(8,128)S(1)}, u32[]{:S(2)}, u32[]{:S(2)}) collective-permute-start(f32[256,128]{1,0:T(8,128)S(1)} %bitcast.6), channel_id=1, source_target_pairs={{32,0},{64,32},{96,64},{128,96},{160,128},{192,160},{224,192},{256... | collective-permute-start | bytes 393224 | tf_op jit(solution)/shard_map/ppermute | solution.py:330
  33.5 10.1 %collective-permute-start.1 = (f32[8,8,8,128]{3,2,1,0:T(8,128)S(1)}, f32[8,8,8,128]{3,2,1,0:T(8,128)S(1)}, u32[]{:S(2)}, u32[]{:S(2)}) collective-permute-start(f32[8,8,8,128]{3,2,1,0:T(8,128)S(1)} %get-tuple-element.13), channel_id=1, source_target_pairs={{0,32},{32,0},{64,96},{96,64},{128,160},{160,128},{192,224},{224,1... | collective-permute-start | bytes 786440 | tf_op jit(solution)/shard_map/ppermute | solution.py:333

commit v6 on v5

--- a/solution.py
+++ b/solution.py
@@ -196,8 +196,8 @@
         own = ref[pl.ds(tile_index * 8 + at, 1), :]
         return jnp.broadcast_to(own[:, tile:tile + 1], (8, LANES))
 
-    def out_copy(s, tile):
-        return pltpu.make_async_copy(out_ref.at[tile], images_ref.at[s, tile], sems.at[tile])
+    def out_copy(tile):
+        return pltpu.make_async_copy(out_ref.at[tile], images_ref.at[1, tile], sems.at[tile])
 
     def finish(s, block):
         for quarter in range(2):
@@ -235,49 +235,45 @@
                     send_ref[z, upper] = jnp.where(core == 0, power_up[1], power_up[0])
                     keep_ref[7 - z, lower] = jnp.where(core == 0, power_down[1], power_down[0])
                     send_ref[7 - z, lower] = jnp.where(core == 0, power_down[0], power_down[1])
-
-    def leave(s, block):
-        for tile in range(block * 4, block * 4 + 4):
-            out_copy(s, tile).start()
+            if s == 1:
+                out_copy(upper).start()
+                out_copy(lower).start()
 
     def last_product(half, block):
         columns = slice(block * 256, block * 256 + 256)
         prods[half][:, columns] = product(*sides[half % 2], slice(0, 2 * DEPTH), columns)
 
-    return stage, last_product, finish, leave, out_copy
-
-
-def first_kernel(tile_ref, g_ref, images_ref, second_ref, power_ref,
-                 left_a, left_b, right_a, right_b, wave_ref, table_ref, prod_ref, out_ref, sems):
-    stage, last_product, finish, leave, out_copy = steps(
+    return stage, last_product, finish, out_copy
+
+
+def first_kernel(tile_ref, g_ref, early_ref, second_ref, power_ref,
+                 left_a, left_b, right_a, right_b, wave_ref, table_ref, prod_ref):
+    stage, last_product, finish, _ = steps(
         tile_ref, None, g_ref, None, ((left_a, right_a), (left_b, right_b)), wave_ref, table_ref,
-        (prod_ref, second_ref), images_ref, out_ref, power_ref, sems)
+        (prod_ref, second_ref), None, early_ref, power_ref, None)
     stage(None, 0)
     stage(0, 1)
     last_product(1, 0)
     last_product(1, 1)
     finish(0, 0)
-    leave(0, 0)
     finish(0, 1)
-    leave(0, 1)
-    for tile in range(TILES_DEV):
-        out_copy(0, tile).wait()
-
-
-def second_kernel(tile_ref, sub_ref, g_ref, next_ref, second_ref, power_ref, before_ref, images_ref, keep_ref, send_ref,
+
+
+def second_kernel(tile_ref, sub_ref, g_ref, next_ref, second_ref, power_ref, early_ref, images_ref, keep_ref, send_ref,
                   left_ref, right_ref, wave_ref, table_ref, prod_ref, out_ref, sems):
-    stage, last_product, finish, leave, out_copy = steps(
+    stage, last_product, finish, out_copy = steps(
         tile_ref, sub_ref, g_ref, next_ref, ((left_ref, right_ref),), wave_ref, table_ref,
         (None, second_ref, prod_ref), images_ref, out_ref, power_ref, sems, keep_ref, send_ref)
+    early = pltpu.make_async_copy(early_ref, images_ref.at[0], sems.at[TILES_DEV])
+    early.start()
     stage(None, 2)
     last_product(2, 0)
     last_product(2, 1)
     finish(1, 0)
-    leave(1, 0)
     finish(1, 1)
-    leave(1, 1)
+    early.wait()
     for tile in range(TILES_DEV):
-        out_copy(1, tile).wait()
+        out_copy(tile).wait()
 
 
 def scratch(sides):
@@ -287,38 +283,35 @@
         pltpu.VMEM((32, LANES), F32),
         pltpu.VMEM((18 * 32, LANES), F32),
         pltpu.VMEM((2 * DEPTH, 512), F32),
-        pltpu.VMEM((TILES_DEV, PIX, 2 * PIX), F32),
-        pltpu.SemaphoreType.DMA((TILES_DEV,)),
     ]
 
 
 def first(tile, gathered):
-    vmem, smem, anywhere = (pl.BlockSpec(memory_space=space) for space in (pltpu.VMEM, pltpu.SMEM, pl.ANY))
+    vmem, smem = (pl.BlockSpec(memory_space=space) for space in (pltpu.VMEM, pltpu.SMEM))
     return pl.pallas_call(
         first_kernel,
-        out_shape=(jax.ShapeDtypeStruct((2, TILES_DEV, PIX, 2 * PIX), F32),
+        out_shape=(jax.ShapeDtypeStruct((TILES_DEV, PIX, 2 * PIX), F32),
                    jax.ShapeDtypeStruct((2 * DEPTH, 512), F32),
                    jax.ShapeDtypeStruct((TILES_DEV, PIX, PIX), F32)),
         in_specs=[smem, vmem],
-        out_specs=(anywhere, vmem, vmem),
+        out_specs=(vmem, vmem, vmem),
         scratch_shapes=scratch(2),
         cost_estimate=pl.CostEstimate(flops=2 * 2 * 512 * 512 * 2048, bytes_accessed=8 << 20, transcendentals=0),
         compiler_params=pltpu.CompilerParams(vmem_limit_bytes=32 * 1024 * 1024),
     )(tile, gathered)
 
 
-def second(tile, sub, gathered, following, product, power, images):
+def second(tile, sub, gathered, following, product, power, early):
     vmem, smem, anywhere = (pl.BlockSpec(memory_space=space) for space in (pltpu.VMEM, pltpu.SMEM, pl.ANY))
     piece = jax.ShapeDtypeStruct((8, TILES_DEV, 8, LANES), F32)
     return pl.pallas_call(
         second_kernel,
         out_shape=(jax.ShapeDtypeStruct((2, TILES_DEV, PIX, 2 * PIX), F32), piece, piece),
-        in_specs=[smem, smem, vmem, vmem, vmem, vmem, anywhere],
+        in_specs=[smem, smem] + [vmem] * 5,
         out_specs=(anywhere, vmem, vmem),
-        scratch_shapes=scratch(1),
-        input_output_aliases={6: 0},
+        scratch_shapes=scratch(1) + [pltpu.VMEM((TILES_DEV, PIX, 2 * PIX), F32), pltpu.SemaphoreType.DMA((TILES_DEV + 1,))],
         compiler_params=pltpu.CompilerParams(vmem_limit_bytes=32 * 1024 * 1024),
-    )(tile, sub, gathered, following, product, power, images)
+    )(tile, sub, gathered, following, product, power, early)
 
 
 def on_device(echoes, pulse_offset, range_gates, visible):
@@ -328,8 +321,8 @@
     own = pack(sub, echoes[:, 0], pulse_offset.reshape(1, 2), range_gates[:, 0], visible)
     gathered = lax.all_to_all(own, "tile", 0, 0, tiled=True).reshape(256, LANES)
     following = lax.ppermute(gathered, "sub", [((i + 1) % subs, i) for i in range(subs)])
-    images, product, power = first(tile, gathered)
-    images, keep, send = second(tile, sub, gathered, following, product, power, images)
+    early, product, power = first(tile, gathered)
+    images, keep, send = second(tile, sub, gathered, following, product, power, early)
     other = lax.ppermute(send, "sub", [(i, i ^ 1) for i in range(subs)])
     both = jnp.maximum(keep, other)
     groups = [[2 * z + c for z in range(subs // 2)] for c in range(2)]

time: 60 us -> 58.9 us (0.982)
  Pallas kernels: 10.9 us -> 9.82 us
    pallas_call x1, Pallas kernels: 5.56 us -> 4.53 us  [first(): pl.pallas_call(first_kernel, out_shape=(jax.ShapeDtypeStruct((TILES_DEV,...]
  transfers between devices with their start and end apart: 3 -> 3, of which waited for: 2 -> 3; matrix products, arithmetic and copies ran while one was open for 0% -> 0% of each run, Pallas kernels for 9% -> 8%
where the time goes in v6:
time: 58.9 us; the launch traced here: 58.6 us
  starting transfers between devices  21.5 us (37%)
  blocking collectives  15.4 us (26%)
  waiting for transfers between devices  10.6 us (18%)
  Pallas kernels  9.82 us (17%)
  between operations  0.68 us (1%)
  other arithmetic  0.67 us (1%)
    all_to_all x1, blocking collectives, on_device(): lax.all_to_all(both, 'sub', 0, 0, tiled=True, axis_index_groups=groups)  15.4 us
    all_to_all x1, starting transfers between devices, on_device(): gathered = lax.all_to_all(own, 'tile', 0, 0, tiled=True).reshape(256, LANES)  10.5 us
    all_to_all x1, waiting for transfers between devices, on_device(): gathered = lax.all_to_all(own, 'tile', 0, 0, tiled=True).reshape(256, LANES)  9.35 us
    ppermute x1, starting transfers between devices, on_device(): other = lax.ppermute(send, 'sub', [(i, i ^ 1) for i in range(subs)])  8.93 us
    pallas_call x1, Pallas kernels, first(): pl.pallas_call(first_kernel, out_shape=(jax.ShapeDtypeStruct((TILES_DEV,...  4.53 us
    pallas_call x1, Pallas kernels, second(): pl.pallas_call(second_kernel, out_shape=(jax.ShapeDtypeStruct((2, TILES_D...  3.69 us
    ppermute x1, starting transfers between devices, on_device(): lax.ppermute(gathered, 'sub', [((i + 1) % subs, i) for i in range(subs)])  2.06 us
    pallas_call x1, Pallas kernels, pack(): pl.pallas_call(pack_kernel, out_shape=jax.ShapeDtypeStruct((32, 8, LANES)...  1.59 us
  transfers between devices with their start and end apart: 3, of which 3 were waited for; matrix products, arithmetic and copies ran while one was open for 0% of the time, Pallas kernels for 8%

profile of v6, /device:TPU:1, one launch (start us, length us, event | category | flops | bytes accessed | tf_op | source)
XLA Modules:
  0.0 58.6 jit_solution(12467133104175765481)
XLA Ops:
  0.6 1.6 %shard_map.59 = f32[32,8,128]{2,1,0:T(8,128)} custom-call(s32[1]{0:T(128)} %bitcast.1.sub_ref, f32[2,128]{1,0:T(2,128)} %bitcast.9, f32[1,2]{1,0:T(1,128)} %bitcast.11, s32[2,64]{1,0:T(2,128)} %bitcast.10, s32[2,8]{1,0:T(2,128)} %shown_hbm.1), custom_call_target="tpu_custom_call" | custom-call | tf_op jit(solution)/shard_map/pallas_call | solution.py:76
  2.2 10.5 %all-to-all-start = ((f32[32,8,128]{2,1,0:T(8,128)}), f32[32,8,128]{2,1,0:T(8,128)S(1)}, u32[]{:S(2)}, u32[]{:S(2)}) async-start(f32[32,8,128]{2,1,0:T(8,128)} %shard_map.59), calls=%async_computation | async-start | bytes 262144 | tf_op jit(solution)/shard_map/all_to_all | solution.py:322
  12.7 9.3 %all-to-all-done = f32[32,8,128]{2,1,0:T(8,128)S(1)} async-done(((f32[32,8,128]{2,1,0:T(8,128)}), f32[32,8,128]{2,1,0:T(8,128)S(1)}, u32[]{:S(2)}, u32[]{:S(2)}) %all-to-all-start) | async-done | bytes 131104 | tf_op jit(solution)/shard_map/all_to_all | solution.py:322
  22.1 2.1 %collective-permute-start = (f32[256,128]{1,0:T(8,128)S(1)}, f32[256,128]{1,0:T(8,128)S(1)}, u32[]{:S(2)}, u32[]{:S(2)}) collective-permute-start(f32[256,128]{1,0:T(8,128)S(1)} %bitcast.6), channel_id=1, source_target_pairs={{32,0},{64,32},{96,64},{128,96},{160,128},{192,160},{224,192},{256... | collective-permute-start | bytes 393224 | tf_op jit(solution)/shard_map/ppermute | solution.py:323
  24.2 4.5 %shard_map.60 = (f32[8,128,256]{2,1,0:T(8,128)S(1)}, f32[512,512]{1,0:T(8,128)S(1)}, f32[8,128,128]{2,1,0:T(8,128)S(1)}) custom-call(s32[1]{0:T(128)} %bitcast.tile_ref, f32[256,128]{1,0:T(8,128)S(1)} %bitcast.7), custom_call_target="tpu_custom_call" | custom-call | flops 2147483648 | bytes 8388608 | tf_op jit(solution)/shard_map/pallas_call | solution.py:291
  28.7 0.1 collective-permute-done.next_ref
  28.8 3.7 %shard_map.61 = (f32[2,8,128,256]{3,2,1,0:T(8,128)}, f32[8,8,8,128]{3,2,1,0:T(8,128)S(1)}, f32[8,8,8,128]{3,2,1,0:T(8,128)S(1)}) custom-call(s32[1]{0:T(128)} %bitcast.tile_ref, s32[1]{0:T(128)} %bitcast.1.sub_ref, f32[256,128]{1,0:T(8,128)S(1)} %bitcast.8, f32[256,128]{1,0:T(8,128)S(1)} %collective-permute-done.next_ref, ...), custom_call_target="tpu_custom_call" | custom-call | tf_op jit(solution)/shard_map/pallas_call | solution.py:307
  32.5 8.9 %collective-permute-start.1 = (f32[8,8,8,128]{3,2,1,0:T(8,128)S(1)}, f32[8,8,8,128]{3,2,1,0:T(8,128)S(1)}, u32[]{:S(2)}, u32[]{:S(2)}) collective-permute-start(f32[8,8,8,128]{3,2,1,0:T(8,128)S(1)} %get-tuple-element.13), channel_id=1, source_target_pairs={{0,32},{32,0},{64,96},{96,64},{128,160},{160,128},{192,224},{224,1... | collective-permute-start | bytes 786440 | tf_op jit(solution)/shard_map/ppermute | solution.py:326
  41.4 1.1 %collective-permute-done.1 = f32[8,8,8,128]{3,2,1,0:T(8,128)S(1)} collective-permute-done((f32[8,8,8,128]{3,2,1,0:T(8,128)S(1)}, f32[8,8,8,128]{3,2,1,0:T(8,128)S(1)}, u32[]{:S(2)}, u32[]{:S(2)}) %collective-permute-start.1) | collective-permute-done | bytes 262176 | tf_op jit(solution)/shard_map/ppermute | solution.py:326
  42.6 15.4 %all_to_all.10 = f32[8,8,8,128]{3,2,1,0:T(8,128)S(1)} all-to-all(f32[8,8,8,128]{3,2,1,0:T(8,128)S(1)} %max.3), channel_id=1, replica_groups={{0,64,128,192,256,320,384,448},{32,96,160,224,288,352,416,480},{1,65,12..., dimensions={0} | all-to-all | bytes 524288 | tf_op jit(solution)/shard_map/all_to_all | solution.py:329
  58.0 0.6 %reduce_max.9 = f32[8,8,128]{2,1,0:T(8,128)} reduce(f32[8,8,8,128]{3,2,1,0:T(8,128)S(1)} %all_to_all.10, f32[]{:T(128)} %constant.10.clone.1), dimensions={0}, to_apply=%region_0.0 | reduce | flops 57344 | bytes 294916 | tf_op jit(solution)/shard_map/reduce_max | solution.py:330
  (1 shorter events, 0.0 us)
Async XLA Ops:
  2.2 19.9 %all-to-all-start = ((f32[32,8,128]{2,1,0:T(8,128)}), f32[32,8,128]{2,1,0:T(8,128)S(1)}, u32[]{:S(2)}, u32[]{:S(2)}) async-start(f32[32,8,128]{2,1,0:T(8,128)} %shard_map.59), calls=%async_computation | async-start | bytes 262144 | tf_op jit(solution)/shard_map/all_to_all | solution.py:322
  22.1 6.7 %collective-permute-start = (f32[256,128]{1,0:T(8,128)S(1)}, f32[256,128]{1,0:T(8,128)S(1)}, u32[]{:S(2)}, u32[]{:S(2)}) collective-permute-start(f32[256,128]{1,0:T(8,128)S(1)} %bitcast.6), channel_id=1, source_target_pairs={{32,0},{64,32},{96,64},{128,96},{160,128},{192,160},{224,192},{256... | collective-permute-start | bytes 393224 | tf_op jit(solution)/shard_map/ppermute | solution.py:323
  32.5 10.1 %collective-permute-start.1 = (f32[8,8,8,128]{3,2,1,0:T(8,128)S(1)}, f32[8,8,8,128]{3,2,1,0:T(8,128)S(1)}, u32[]{:S(2)}, u32[]{:S(2)}) collective-permute-start(f32[8,8,8,128]{3,2,1,0:T(8,128)S(1)} %get-tuple-element.13), channel_id=1, source_target_pairs={{0,32},{32,0},{64,96},{96,64},{128,160},{160,128},{192,224},{224,1... | collective-permute-start | bytes 786440 | tf_op jit(solution)/shard_map/ppermute | solution.py:326
